TPU v7x, 32 devices: a whole 2x2x4 slice. The times are simulated.
32 devices in a mesh: pipe: 4 (over y, x), dp: 4 (over z), tensor: 2 (over core).
Axes of the slice: x: 2, y: 2, z: 4, core: 2. Of those that a mesh axis runs over, the one named last changes fastest.
Arguments:
- llm_grad: bfloat16 [4, 128, 1664], P(None, 'dp'), may hold values from -6 to 6
- slot_row: int32 [4, 4, 32], P(None, 'dp'), may hold values from 0 to 31, each once within a row
- counts: int32 [4, 4], P('dp'), may hold values from 8 to 32, as said below
- saved_in: bfloat16 [4, 4, 128, 1664], P('pipe', None, 'dp'), may hold values from -6 to 6
- saved_pre: bfloat16 [4, 4, 128, 6400], P('pipe', None, 'dp', 'tensor'), may hold values from -6 to 6
- weights: bfloat16 [4, 1664, 6400], P('pipe', 'dp', 'tensor'), may hold values from -0.15625 to 0.15625
- channel_scale: float32 [4, 1664], P('pipe'), may hold values from 0.25 to 2
Outputs:
- weight_grad: bfloat16 [4, 1664, 6400], P('pipe', 'dp', 'tensor')
- section_grad: bfloat16 [4, 4, 128, 1664], P('pipe', None, 'dp')
Inputs may be any that keep to these rules, and one draw needn't show every extreme that they name: For each micro-batch and rank, slot_row lists every row of the rank once. `counts`: both ends of the range occur in every draw.
All inputs are finite; a program needn't handle non-finite values.
Results may differ from a plain program's by a relative error of at most 0.023.
Values may be sent and summed in bfloat16 or wider, within the bound.
No kernel may reach another device: no remote copies, remote signals or barrier semaphores. Data moves between devices by JAX's collectives and lax.ppermute only.
A program may use at most 128 MiB of HBM per device.

v0:
```python
import jax
import jax.numpy as jnp
from jax import lax
from jax.sharding import PartitionSpec as P

norm_eps = 1e-06
root_half = 0.7071067811865476
inv_root_two_pi = 0.3989422804014327


def shortened(value):

    def short(part):
        return part.astype(jnp.bfloat16) if part.dtype == jnp.float32 else part

    return jax.tree.map(short, value)


def shifted(block, axis, distance):
    devices = range(lax.axis_size(axis))
    route = [(i - distance, i) for i in devices if i - distance in devices]
    return lax.ppermute(block, axis, route)


def gelu_parts(pre_act):
    normal_cdf = 0.5 * (1.0 + jax.scipy.special.erf(pre_act * root_half))
    density = jnp.exp(-0.5 * pre_act * pre_act) * inv_root_two_pi
    return (pre_act * normal_cdf, normal_cdf + pre_act * density)


def local_top(llm_grad, slot_row, counts):
    row_count = llm_grad.shape[1]
    slot_ids = jnp.arange(row_count, dtype=jnp.int32)
    kept_mask = slot_ids[None, :] < counts[:, None]
    source = jnp.where(kept_mask[..., None], llm_grad, jnp.zeros_like(llm_grad))
    onehot = (slot_row[:, :, None] == slot_ids[None, None, :]).astype(jnp.bfloat16)
    placed = jnp.einsum("mjr,mjd->mrd", onehot, source, preferred_element_type=jnp.float32)
    return placed.astype(jnp.bfloat16)


def norm_back(incoming, dnorm, unit_rows, inv_std, channel_gain):
    scaled_back = dnorm * channel_gain
    back = inv_std * (
        scaled_back
        - jnp.mean(scaled_back, axis=-1, keepdims=True)
        - unit_rows * jnp.mean(scaled_back * unit_rows, axis=-1, keepdims=True)
    )
    return (incoming.astype(jnp.float32) + back).astype(jnp.bfloat16)


def body(llm_grad, slot_row, counts, saved_in, saved_pre, weights, channel_scale):
    sections = lax.axis_size("pipe")
    section_index = lax.axis_index("pipe")
    micro_count = llm_grad.shape[0]
    row_count = llm_grad.shape[1]
    model_width = llm_grad.shape[2]
    hidden = saved_pre.shape[3]
    is_up = section_index % 2 == 0
    is_top = section_index == sections - 1
    full_weight = lax.all_gather(weights[0], "dp", axis=0, tiled=True)
    channel_gain = channel_scale[0]
    top_grad = local_top(llm_grad, slot_row[:, 0], counts[0])
    zero_wide = jnp.zeros((row_count, model_width), jnp.float32)
    zero_narrow = jnp.zeros((row_count, model_width), jnp.bfloat16)
    zero_hidden = jnp.zeros((row_count, hidden), jnp.bfloat16)

    def spare_work(incoming, hidden_in, inputs, pre_act):
        return (zero_wide, zero_hidden, zero_narrow, zero_hidden)

    def down_work(incoming, hidden_in, inputs, pre_act):
        scaled = (incoming.astype(jnp.float32) * channel_gain).astype(jnp.bfloat16)
        hidden_grad = jnp.dot(scaled, full_weight, preferred_element_type=jnp.float32).astype(
            jnp.bfloat16
        )
        activated = gelu_parts(pre_act.astype(jnp.float32))[0].astype(jnp.bfloat16)
        return (zero_wide, hidden_grad, scaled, activated)

    def up_work(incoming, hidden_in, inputs, pre_act):
        act_grad = (
            hidden_in.astype(jnp.float32) * gelu_parts(pre_act.astype(jnp.float32))[1]
        ).astype(jnp.bfloat16)
        values = inputs.astype(jnp.float32)
        center = values - jnp.mean(values, axis=-1, keepdims=True)
        inv_std = lax.rsqrt(jnp.mean(center * center, axis=-1, keepdims=True) + norm_eps)
        normed = (center * inv_std * channel_gain).astype(jnp.bfloat16)
        partial_value = lax.dot_general(
            act_grad, full_weight, (((1,), (1,)), ((), ())), preferred_element_type=jnp.float32
        )
        return (partial_value, zero_hidden, normed, act_grad)

    def advance(loop_state, tick_index):
        grad_store, out_buffer, recv_hidden, recv_res = loop_state
        micro_index = tick_index - (sections - 1 - section_index)
        is_valid = (micro_index >= 0) & (micro_index < micro_count)
        micro_safe = jnp.clip(micro_index, 0, micro_count - 1)
        incoming = jnp.where(is_top, top_grad[micro_safe], recv_res)
        inputs = saved_in[0, micro_safe]
        pre_act = saved_pre[0, micro_safe]
        branch = jnp.where(is_valid, jnp.where(is_up, 2, 1), 0).astype(jnp.int32)
        partial_value, hidden_out, left_side, right_side = lax.switch(
            branch, [spare_work, down_work, up_work], incoming, recv_hidden, inputs, pre_act
        )
        values = inputs.astype(jnp.float32)
        center = values - jnp.mean(values, axis=-1, keepdims=True)
        inv_std = lax.rsqrt(jnp.mean(center * center, axis=-1, keepdims=True) + norm_eps)
        unit_rows = center * inv_std
        summed = jax.tree.map(
            lambda part: part.astype(jnp.float32), lax.psum(shortened(partial_value), "tensor")
        )
        back_out = norm_back(incoming, summed, unit_rows, inv_std, channel_gain)
        outgoing = jnp.where(is_up, back_out, incoming)
        write_at = jnp.where(is_valid, micro_safe, micro_count)
        out_buffer = lax.dynamic_update_index_in_dim(out_buffer, outgoing, write_at, 0)
        left_buffer, right_buffer = grad_store
        left_buffer = lax.dynamic_update_index_in_dim(left_buffer, left_side, write_at, 0)
        right_buffer = lax.dynamic_update_index_in_dim(right_buffer, right_side, write_at, 0)
        grad_store = (left_buffer, right_buffer)
        recv_hidden, recv_res = (
            shifted(shortened(hidden_out), "pipe", -1).astype(hidden_out.dtype),
            shifted(outgoing, "pipe", -1),
        )
        return ((grad_store, out_buffer, recv_hidden, recv_res), None)

    grad_store = (
        jnp.zeros((micro_count + 1, row_count, model_width), jnp.bfloat16),
        jnp.zeros((micro_count + 1, row_count, hidden), jnp.bfloat16),
    )
    out_buffer = jnp.zeros((micro_count + 1, row_count, model_width), jnp.bfloat16)
    tick_count = micro_count + sections - 1
    loop_state = (grad_store, out_buffer, zero_hidden, zero_narrow)
    loop_state, unused = lax.scan(advance, loop_state, jnp.arange(tick_count, dtype=jnp.int32))
    grad_store, out_buffer, recv_hidden, recv_res = loop_state
    left_buffer, right_buffer = grad_store
    flat_left = left_buffer[:micro_count].reshape(micro_count * row_count, model_width)
    flat_right = right_buffer[:micro_count].reshape(micro_count * row_count, hidden)
    weight_out = lax.psum_scatter(
        lax.dot_general(
            flat_left, flat_right, (((0,), (0,)), ((), ())), preferred_element_type=jnp.float32
        ).astype(jnp.bfloat16),
        "dp",
        scatter_dimension=0,
        tiled=True,
    )
    return (weight_out[None], out_buffer[:micro_count][None])


def solution(mesh):
    in_specs = (
        P(None, "dp", None),
        P(None, "dp", None),
        P("dp", None),
        P("pipe", None, "dp", None),
        P("pipe", None, "dp", "tensor"),
        P("pipe", "dp", "tensor"),
        P("pipe", None),
    )
    out_specs = (P("pipe", "dp", "tensor"), P("pipe", None, "dp", None))
    return jax.shard_map(body, mesh=mesh, in_specs=in_specs, out_specs=out_specs, check_vma=False)
```

profile of v0, /device:TPU:0, one launch (start us, length us, event | category | flops | bytes accessed | tf_op | source)
XLA Modules:
  0.0 668.3 jit_solution(7804911929858855091)
XLA Ops:
  8.6 1.4 convolution_convert_fusion.1
  10.0 188.9 %all-gather.3.cloned.1.call-done = bf16[1,1664,3200]{2,1,0:T(8,128)(2,1)} async-done(((bf16[1,416,3200]{2,1,0:T(8,128)(2,1)}), bf16[1,1664,3200]{2,1,0:T(8,128)(2,1)}) %all-gather.3.cloned.1.call-update) | async-done | bytes 10649616 | tf_op jit(solution)/shard_map/all_gather | solution.py:60
  199.9 271.5 %while.20 = (s32[]{:T(128)}, bf16[5,32,1664]{2,1,0:T(8,128)(2,1)}, bf16[5,32,3200]{2,1,0:T(8,128)(2,1)S(1)}, bf16[5,32,1664]{2,1,0:T(8,128)(2,1)S(1)}, bf16[32,3...) while((s32[]{:T(128)}, bf16[5,32,1664]{2,1,0:T(8,128)(2,1)}, ...), condition=%wide.region_11.12_spmd, body=%wide.region_0.11_spmd.sunk | while | flops 345374784 | bytes 17218160 | solution.py:131
  204.0 1.3 collective-permute-start
  206.3 20.6 %all-reduce.2.cloned.1.call-done = bf16[32,1664]{1,0:T(8,128)(2,1)} async-done(((bf16[32,1664]{1,0:T(8,128)(2,1)}), bf16[32,1664]{1,0:T(8,128)(2,1)}) %all-reduce.2.cloned.1.call-update) | async-done | bytes 106512 | tf_op jit(solution)/shard_map/while/body/eval_jaxpr/psum | solution.py:108
  231.0 5.2 collective-permute-done.1
  240.2 1.3 collective-permute-start
  242.5 23.8 %all-reduce.2.cloned.1.call-done = bf16[32,1664]{1,0:T(8,128)(2,1)} async-done(((bf16[32,1664]{1,0:T(8,128)(2,1)}), bf16[32,1664]{1,0:T(8,128)(2,1)}) %all-reduce.2.cloned.1.call-update) | async-done | bytes 106512 | tf_op jit(solution)/shard_map/while/body/eval_jaxpr/psum | solution.py:108
  270.4 5.2 collective-permute-done.1
  279.6 1.3 collective-permute-start
  281.9 23.8 %all-reduce.2.cloned.1.call-done = bf16[32,1664]{1,0:T(8,128)(2,1)} async-done(((bf16[32,1664]{1,0:T(8,128)(2,1)}), bf16[32,1664]{1,0:T(8,128)(2,1)}) %all-reduce.2.cloned.1.call-update) | async-done | bytes 106512 | tf_op jit(solution)/shard_map/while/body/eval_jaxpr/psum | solution.py:108
  309.8 5.2 collective-permute-done.1
  318.2 7.9 %conditional.2 = (bf16[32,1664]{1,0:T(8,128)(2,1)S(1)}, bf16[32,3200]{1,0:T(8,128)(2,1)S(1)}, bf16[1,32,1664]{2,1,0:T(8,128)(2,1)S(1)}, bf16[1,32,3200]{2,1,0:T(8,128)(2,1)S(1)}) conditional(s32[]{:T(128)} %clamp.6, () %tuple.62, (bf16[32,1664]{1,0:T(8,128)(2,1)S(1)}, f32[1,1664]{1,0:T(1,128)}, bf16[1664,3200]{1,0:T(8,128)(2,1)}, ...), branch_computations={%region_1.1_spmd, %region_2.2_spmd, %region_3.5_spmd} | conditional | flops 343830560 | bytes 12458690 | solution.py:100
  318.2 7.1 %fusion.21 = bf16[32,1664]{1,0:T(8,128)(2,1)S(1)} fusion(bf16[1664,3200]{1,0:T(8,128)(2,1)} %get-tuple-element.187, bf16[32,3200]{1,0:T(8,128)(2,1)S(1)} %get-tuple-element.186, bf16[32,3200]{1,0:T(8,128)(2,1)S(1)} %get-tuple-element.185), kind=kOutput, calls=%fused_computation.33 | convolution fusion | flops 342016000 | bytes 11165696 | tf_op jit(solution)/shard_map/while/body/eval_jaxpr/cond/branch_2_fun/dot_general | solution.py:86
  329.1 15.9 %all-reduce.2.cloned.1.call-done = bf16[32,1664]{1,0:T(8,128)(2,1)} async-done(((bf16[32,1664]{1,0:T(8,128)(2,1)}), bf16[32,1664]{1,0:T(8,128)(2,1)}) %all-reduce.2.cloned.1.call-update) | async-done | bytes 106512 | tf_op jit(solution)/shard_map/while/body/eval_jaxpr/psum | solution.py:108
  349.2 5.2 collective-permute-done.1
  357.6 7.9 %conditional.2 = (bf16[32,1664]{1,0:T(8,128)(2,1)S(1)}, bf16[32,3200]{1,0:T(8,128)(2,1)S(1)}, bf16[1,32,1664]{2,1,0:T(8,128)(2,1)S(1)}, bf16[1,32,3200]{2,1,0:T(8,128)(2,1)S(1)}) conditional(s32[]{:T(128)} %clamp.6, () %tuple.62, (bf16[32,1664]{1,0:T(8,128)(2,1)S(1)}, f32[1,1664]{1,0:T(1,128)}, bf16[1664,3200]{1,0:T(8,128)(2,1)}, ...), branch_computations={%region_1.1_spmd, %region_2.2_spmd, %region_3.5_spmd} | conditional | flops 343830560 | bytes 12458690 | solution.py:100
  357.6 7.1 %fusion.21 = bf16[32,1664]{1,0:T(8,128)(2,1)S(1)} fusion(bf16[1664,3200]{1,0:T(8,128)(2,1)} %get-tuple-element.187, bf16[32,3200]{1,0:T(8,128)(2,1)S(1)} %get-tuple-element.186, bf16[32,3200]{1,0:T(8,128)(2,1)S(1)} %get-tuple-element.185), kind=kOutput, calls=%fused_computation.33 | convolution fusion | flops 342016000 | bytes 11165696 | tf_op jit(solution)/shard_map/while/body/eval_jaxpr/cond/branch_2_fun/dot_general | solution.py:86
  366.2 1.3 collective-permute-start
  368.5 15.9 %all-reduce.2.cloned.1.call-done = bf16[32,1664]{1,0:T(8,128)(2,1)} async-done(((bf16[32,1664]{1,0:T(8,128)(2,1)}), bf16[32,1664]{1,0:T(8,128)(2,1)}) %all-reduce.2.cloned.1.call-update) | async-done | bytes 106512 | tf_op jit(solution)/shard_map/while/body/eval_jaxpr/psum | solution.py:108
  388.6 5.2 collective-permute-done.1
  397.0 7.9 %conditional.2 = (bf16[32,1664]{1,0:T(8,128)(2,1)S(1)}, bf16[32,3200]{1,0:T(8,128)(2,1)S(1)}, bf16[1,32,1664]{2,1,0:T(8,128)(2,1)S(1)}, bf16[1,32,3200]{2,1,0:T(8,128)(2,1)S(1)}) conditional(s32[]{:T(128)} %clamp.6, () %tuple.62, (bf16[32,1664]{1,0:T(8,128)(2,1)S(1)}, f32[1,1664]{1,0:T(1,128)}, bf16[1664,3200]{1,0:T(8,128)(2,1)}, ...), branch_computations={%region_1.1_spmd, %region_2.2_spmd, %region_3.5_spmd} | conditional | flops 343830560 | bytes 12458690 | solution.py:100
  397.0 7.1 %fusion.21 = bf16[32,1664]{1,0:T(8,128)(2,1)S(1)} fusion(bf16[1664,3200]{1,0:T(8,128)(2,1)} %get-tuple-element.187, bf16[32,3200]{1,0:T(8,128)(2,1)S(1)} %get-tuple-element.186, bf16[32,3200]{1,0:T(8,128)(2,1)S(1)} %get-tuple-element.185), kind=kOutput, calls=%fused_computation.33 | convolution fusion | flops 342016000 | bytes 11165696 | tf_op jit(solution)/shard_map/while/body/eval_jaxpr/cond/branch_2_fun/dot_general | solution.py:86
  407.8 15.7 %all-reduce.2.cloned.1.call-done = bf16[32,1664]{1,0:T(8,128)(2,1)} async-done(((bf16[32,1664]{1,0:T(8,128)(2,1)}), bf16[32,1664]{1,0:T(8,128)(2,1)}) %all-reduce.2.cloned.1.call-update) | async-done | bytes 106512 | tf_op jit(solution)/shard_map/while/body/eval_jaxpr/psum | solution.py:108
  427.7 5.2 collective-permute-done.1
  436.2 7.9 %conditional.2 = (bf16[32,1664]{1,0:T(8,128)(2,1)S(1)}, bf16[32,3200]{1,0:T(8,128)(2,1)S(1)}, bf16[1,32,1664]{2,1,0:T(8,128)(2,1)S(1)}, bf16[1,32,3200]{2,1,0:T(8,128)(2,1)S(1)}) conditional(s32[]{:T(128)} %clamp.6, () %tuple.62, (bf16[32,1664]{1,0:T(8,128)(2,1)S(1)}, f32[1,1664]{1,0:T(1,128)}, bf16[1664,3200]{1,0:T(8,128)(2,1)}, ...), branch_computations={%region_1.1_spmd, %region_2.2_spmd, %region_3.5_spmd} | conditional | flops 343830560 | bytes 12458690 | solution.py:100
  436.2 7.1 %fusion.21 = bf16[32,1664]{1,0:T(8,128)(2,1)S(1)} fusion(bf16[1664,3200]{1,0:T(8,128)(2,1)} %get-tuple-element.187, bf16[32,3200]{1,0:T(8,128)(2,1)S(1)} %get-tuple-element.186, bf16[32,3200]{1,0:T(8,128)(2,1)S(1)} %get-tuple-element.185), kind=kOutput, calls=%fused_computation.33 | convolution fusion | flops 342016000 | bytes 11165696 | tf_op jit(solution)/shard_map/while/body/eval_jaxpr/cond/branch_2_fun/dot_general | solution.py:86
  444.8 1.3 collective-permute-start
  447.0 15.1 %all-reduce.2.cloned.1.call-done = bf16[32,1664]{1,0:T(8,128)(2,1)} async-done(((bf16[32,1664]{1,0:T(8,128)(2,1)}), bf16[32,1664]{1,0:T(8,128)(2,1)}) %all-reduce.2.cloned.1.call-update) | async-done | bytes 106512 | tf_op jit(solution)/shard_map/while/body/eval_jaxpr/psum | solution.py:108
  466.2 5.2 collective-permute-done.1
  471.4 8.0 %bitcast_convert_fusion = bf16[1664,3200]{1,0:T(8,128)(2,1)} fusion(bf16[5,32,1664]{2,1,0:T(8,128)(2,1)} %get-tuple-element.216, bf16[5,32,3200]{2,1,0:T(8,128)(2,1)S(1)} %get-tuple-element.217), kind=kOutput, calls=%fused_computation.59 | convolution fusion | flops 1368473600 | bytes 12001280 | tf_op jit(solution)/shard_map/dot_general | solution.py:137
  480.2 181.6 %reduce-scatter.2.cloned.1.call-done = bf16[416,3200]{1,0:T(8,128)(2,1)} async-done(((bf16[1664,3200]{1,0:T(8,128)(2,1)}), bf16[416,3200]{1,0:T(8,128)(2,1)}) %reduce-scatter.2.cloned.1.call-update) | async-done | bytes 2662416 | tf_op jit(solution)/shard_map/reduce_scatter | solution.py:136
  (202 shorter events, 67.4 us)
Async XLA Ops:
  7.2 191.7 %all-gather.3.cloned.1.call-start = ((), (), s32[]{:S(2)}) async-start(), calls=%async_computation.2 | async-start | bytes 13312000 | tf_op jit(solution)/shard_map/all_gather | solution.py:60
  199.9 27.0 %all-reduce.2.cloned.1.call-start = ((), (), s32[]{:S(2)}) async-start(), calls=%async_computation.3 | async-start | bytes 212992 | tf_op jit(solution)/shard_map/while/body/eval_jaxpr/psum | solution.py:108
  203.3 0.6 copy-start
  204.0 27.0 %collective-permute-start = (bf16[32,3200]{1,0:T(8,128)(2,1)S(1)}, bf16[32,3200]{1,0:T(8,128)(2,1)S(1)}, u32[]{:S(2)}, u32[]{:S(2)}) collective-permute-start(bf16[32,3200]{1,0:T(8,128)(2,1)S(1)} %get-tuple-element.378), channel_id=1, source_target_pairs={{8,0},{16,8},{24,16},{9,1},{17,9},{25,17},{10,2},{18,10},{26,18},{... | collective-permute-start | bytes 614408 | tf_op jit(solution)/shard_map/while/body/eval_jaxpr/ppermute | solution.py:22
  229.1 7.1 %collective-permute-start.1 = (bf16[32,1664]{1,0:T(8,128)(2,1)S(1)}, bf16[32,1664]{1,0:T(8,128)(2,1)S(1)}, u32[]{:S(2)}, u32[]{:S(2)}) collective-permute-start(bf16[32,1664]{1,0:T(8,128)(2,1)S(1)} %get-tuple-element.379), channel_id=1, source_target_pairs={{8,0},{16,8},{24,16},{9,1},{17,9},{25,17},{10,2},{18,10},{26,18},{... | collective-permute-start | bytes 319496 | tf_op jit(solution)/shard_map/while/body/eval_jaxpr/ppermute | solution.py:22
  236.2 30.1 %all-reduce.2.cloned.1.call-start = ((), (), s32[]{:S(2)}) async-start(), calls=%async_computation.3 | async-start | bytes 212992 | tf_op jit(solution)/shard_map/while/body/eval_jaxpr/psum | solution.py:108
  239.5 0.6 copy-start
  240.2 30.2 %collective-permute-start = (bf16[32,3200]{1,0:T(8,128)(2,1)S(1)}, bf16[32,3200]{1,0:T(8,128)(2,1)S(1)}, u32[]{:S(2)}, u32[]{:S(2)}) collective-permute-start(bf16[32,3200]{1,0:T(8,128)(2,1)S(1)} %get-tuple-element.378), channel_id=1, source_target_pairs={{8,0},{16,8},{24,16},{9,1},{17,9},{25,17},{10,2},{18,10},{26,18},{... | collective-permute-start | bytes 614408 | tf_op jit(solution)/shard_map/while/body/eval_jaxpr/ppermute | solution.py:22
  268.4 7.1 %collective-permute-start.1 = (bf16[32,1664]{1,0:T(8,128)(2,1)S(1)}, bf16[32,1664]{1,0:T(8,128)(2,1)S(1)}, u32[]{:S(2)}, u32[]{:S(2)}) collective-permute-start(bf16[32,1664]{1,0:T(8,128)(2,1)S(1)} %get-tuple-element.379), channel_id=1, source_target_pairs={{8,0},{16,8},{24,16},{9,1},{17,9},{25,17},{10,2},{18,10},{26,18},{... | collective-permute-start | bytes 319496 | tf_op jit(solution)/shard_map/while/body/eval_jaxpr/ppermute | solution.py:22
  275.6 30.1 %all-reduce.2.cloned.1.call-start = ((), (), s32[]{:S(2)}) async-start(), calls=%async_computation.3 | async-start | bytes 212992 | tf_op jit(solution)/shard_map/while/body/eval_jaxpr/psum | solution.py:108
  278.9 0.6 copy-start
  279.6 30.2 %collective-permute-start = (bf16[32,3200]{1,0:T(8,128)(2,1)S(1)}, bf16[32,3200]{1,0:T(8,128)(2,1)S(1)}, u32[]{:S(2)}, u32[]{:S(2)}) collective-permute-start(bf16[32,3200]{1,0:T(8,128)(2,1)S(1)} %get-tuple-element.378), channel_id=1, source_target_pairs={{8,0},{16,8},{24,16},{9,1},{17,9},{25,17},{10,2},{18,10},{26,18},{... | collective-permute-start | bytes 614408 | tf_op jit(solution)/shard_map/while/body/eval_jaxpr/ppermute | solution.py:22
  307.8 7.1 %collective-permute-start.1 = (bf16[32,1664]{1,0:T(8,128)(2,1)S(1)}, bf16[32,1664]{1,0:T(8,128)(2,1)S(1)}, u32[]{:S(2)}, u32[]{:S(2)}) collective-permute-start(bf16[32,1664]{1,0:T(8,128)(2,1)S(1)} %get-tuple-element.379), channel_id=1, source_target_pairs={{8,0},{16,8},{24,16},{9,1},{17,9},{25,17},{10,2},{18,10},{26,18},{... | collective-permute-start | bytes 319496 | tf_op jit(solution)/shard_map/while/body/eval_jaxpr/ppermute | solution.py:22
  314.9 30.1 %all-reduce.2.cloned.1.call-start = ((), (), s32[]{:S(2)}) async-start(), calls=%async_computation.3 | async-start | bytes 212992 | tf_op jit(solution)/shard_map/while/body/eval_jaxpr/psum | solution.py:108
  318.2 7.7 %copy-start.1 = (f32[1,1664]{1,0:T(1,128)S(1)}, f32[1,1664]{1,0:T(1,128)}, u32[]{:S(2)}) copy-start(f32[1,1664]{1,0:T(1,128)} %get-tuple-element.189) | copy-start | bytes 19972 | tf_op jit(solution)/shard_map/while/body/eval_jaxpr/cond
  326.8 22.4 %collective-permute-start = (bf16[32,3200]{1,0:T(8,128)(2,1)S(1)}, bf16[32,3200]{1,0:T(8,128)(2,1)S(1)}, u32[]{:S(2)}, u32[]{:S(2)}) collective-permute-start(bf16[32,3200]{1,0:T(8,128)(2,1)S(1)} %get-tuple-element.378), channel_id=1, source_target_pairs={{8,0},{16,8},{24,16},{9,1},{17,9},{25,17},{10,2},{18,10},{26,18},{... | collective-permute-start | bytes 614408 | tf_op jit(solution)/shard_map/while/body/eval_jaxpr/ppermute | solution.py:22
  347.2 7.1 %collective-permute-start.1 = (bf16[32,1664]{1,0:T(8,128)(2,1)S(1)}, bf16[32,1664]{1,0:T(8,128)(2,1)S(1)}, u32[]{:S(2)}, u32[]{:S(2)}) collective-permute-start(bf16[32,1664]{1,0:T(8,128)(2,1)S(1)} %get-tuple-element.379), channel_id=1, source_target_pairs={{8,0},{16,8},{24,16},{9,1},{17,9},{25,17},{10,2},{18,10},{26,18},{... | collective-permute-start | bytes 319496 | tf_op jit(solution)/shard_map/while/body/eval_jaxpr/ppermute | solution.py:22
  354.3 30.1 %all-reduce.2.cloned.1.call-start = ((), (), s32[]{:S(2)}) async-start(), calls=%async_computation.3 | async-start | bytes 212992 | tf_op jit(solution)/shard_map/while/body/eval_jaxpr/psum | solution.py:108
  357.6 7.7 %copy-start.1 = (f32[1,1664]{1,0:T(1,128)S(1)}, f32[1,1664]{1,0:T(1,128)}, u32[]{:S(2)}) copy-start(f32[1,1664]{1,0:T(1,128)} %get-tuple-element.189) | copy-start | bytes 19972 | tf_op jit(solution)/shard_map/while/body/eval_jaxpr/cond
  365.5 0.6 copy-start
  366.2 22.4 %collective-permute-start = (bf16[32,3200]{1,0:T(8,128)(2,1)S(1)}, bf16[32,3200]{1,0:T(8,128)(2,1)S(1)}, u32[]{:S(2)}, u32[]{:S(2)}) collective-permute-start(bf16[32,3200]{1,0:T(8,128)(2,1)S(1)} %get-tuple-element.378), channel_id=1, source_target_pairs={{8,0},{16,8},{24,16},{9,1},{17,9},{25,17},{10,2},{18,10},{26,18},{... | collective-permute-start | bytes 614408 | tf_op jit(solution)/shard_map/while/body/eval_jaxpr/ppermute | solution.py:22
  386.6 7.1 %collective-permute-start.1 = (bf16[32,1664]{1,0:T(8,128)(2,1)S(1)}, bf16[32,1664]{1,0:T(8,128)(2,1)S(1)}, u32[]{:S(2)}, u32[]{:S(2)}) collective-permute-start(bf16[32,1664]{1,0:T(8,128)(2,1)S(1)} %get-tuple-element.379), channel_id=1, source_target_pairs={{8,0},{16,8},{24,16},{9,1},{17,9},{25,17},{10,2},{18,10},{26,18},{... | collective-permute-start | bytes 319496 | tf_op jit(solution)/shard_map/while/body/eval_jaxpr/ppermute | solution.py:22
  393.7 29.9 %all-reduce.2.cloned.1.call-start = ((), (), s32[]{:S(2)}) async-start(), calls=%async_computation.3 | async-start | bytes 212992 | tf_op jit(solution)/shard_map/while/body/eval_jaxpr/psum | solution.py:108
  397.0 7.7 %copy-start.1 = (f32[1,1664]{1,0:T(1,128)S(1)}, f32[1,1664]{1,0:T(1,128)}, u32[]{:S(2)}) copy-start(f32[1,1664]{1,0:T(1,128)} %get-tuple-element.189) | copy-start | bytes 19972 | tf_op jit(solution)/shard_map/while/body/eval_jaxpr/cond
  405.6 22.2 %collective-permute-start = (bf16[32,3200]{1,0:T(8,128)(2,1)S(1)}, bf16[32,3200]{1,0:T(8,128)(2,1)S(1)}, u32[]{:S(2)}, u32[]{:S(2)}) collective-permute-start(bf16[32,3200]{1,0:T(8,128)(2,1)S(1)} %get-tuple-element.378), channel_id=1, source_target_pairs={{8,0},{16,8},{24,16},{9,1},{17,9},{25,17},{10,2},{18,10},{26,18},{... | collective-permute-start | bytes 614408 | tf_op jit(solution)/shard_map/while/body/eval_jaxpr/ppermute | solution.py:22
  425.8 7.1 %collective-permute-start.1 = (bf16[32,1664]{1,0:T(8,128)(2,1)S(1)}, bf16[32,1664]{1,0:T(8,128)(2,1)S(1)}, u32[]{:S(2)}, u32[]{:S(2)}) collective-permute-start(bf16[32,1664]{1,0:T(8,128)(2,1)S(1)} %get-tuple-element.379), channel_id=1, source_target_pairs={{8,0},{16,8},{24,16},{9,1},{17,9},{25,17},{10,2},{18,10},{26,18},{... | collective-permute-start | bytes 319496 | tf_op jit(solution)/shard_map/while/body/eval_jaxpr/ppermute | solution.py:22
  432.9 29.2 %all-reduce.2.cloned.1.call-start = ((), (), s32[]{:S(2)}) async-start(), calls=%async_computation.3 | async-start | bytes 212992 | tf_op jit(solution)/shard_map/while/body/eval_jaxpr/psum | solution.py:108
  436.2 7.7 %copy-start.1 = (f32[1,1664]{1,0:T(1,128)S(1)}, f32[1,1664]{1,0:T(1,128)}, u32[]{:S(2)}) copy-start(f32[1,1664]{1,0:T(1,128)} %get-tuple-element.189) | copy-start | bytes 19972 | tf_op jit(solution)/shard_map/while/body/eval_jaxpr/cond
  444.1 0.6 copy-start
  444.8 21.5 %collective-permute-start = (bf16[32,3200]{1,0:T(8,128)(2,1)S(1)}, bf16[32,3200]{1,0:T(8,128)(2,1)S(1)}, u32[]{:S(2)}, u32[]{:S(2)}) collective-permute-start(bf16[32,3200]{1,0:T(8,128)(2,1)S(1)} %get-tuple-element.378), channel_id=1, source_target_pairs={{8,0},{16,8},{24,16},{9,1},{17,9},{25,17},{10,2},{18,10},{26,18},{... | collective-permute-start | bytes 614408 | tf_op jit(solution)/shard_map/while/body/eval_jaxpr/ppermute | solution.py:22
  464.3 7.1 %collective-permute-start.1 = (bf16[32,1664]{1,0:T(8,128)(2,1)S(1)}, bf16[32,1664]{1,0:T(8,128)(2,1)S(1)}, u32[]{:S(2)}, u32[]{:S(2)}) collective-permute-start(bf16[32,1664]{1,0:T(8,128)(2,1)S(1)} %get-tuple-element.379), channel_id=1, source_target_pairs={{8,0},{16,8},{24,16},{9,1},{17,9},{25,17},{10,2},{18,10},{26,18},{... | collective-permute-start | bytes 319496 | tf_op jit(solution)/shard_map/while/body/eval_jaxpr/ppermute | solution.py:22
  471.4 190.4 %reduce-scatter.2.cloned.1.call-start = ((), (), s32[]{:S(2)}) async-start(), calls=%async_computation.1 | async-start | bytes 13312000 | tf_op jit(solution)/shard_map/reduce_scatter | solution.py:136
  (2 other events, 1.3 us)
Sparse Core Ops, SparseCore 0:
  9.5 189.2 all-gather.2
  204.1 22.7 all-reduce.1
  240.3 25.8 all-reduce.1
  279.7 25.8 all-reduce.1
  326.9 18.0 all-reduce.1
  366.3 18.0 all-reduce.1
  405.7 17.8 all-reduce.1
  444.9 17.1 all-reduce.1
  479.5 182.1 reduce-scatter.1
where the time goes:
time: 670 us; the launch traced here: 668 us
  waiting for transfers between devices  538 us (80%)
  matrix products  37.9 us (6%)
  other arithmetic  32.5 us (5%)
  local copies, waits for them, and re-layouts  22 us (3%)
  starting transfers between devices  18.2 us (3%)
  between operations  13.8 us (2%)
    all_gather x1, waiting for transfers between devices, body(): full_weight = lax.all_gather(weights[0], 'dp', axis=0, tiled=True)  189 us
    reduce_scatter x1, waiting for transfers between devices, body(): lax.psum_scatter(lax.dot_general(flat_left, flat_right, (((0,), (0,)), ((...  182 us
    psum x7, waiting for transfers between devices, advance(): lax.psum(shortened(partial_value), 'tensor')  131 us
    ppermute x14, waiting for transfers between devices, shifted(): return lax.ppermute(block, axis, route)  36.1 us
    dot_general x4, matrix products, up_work(): lax.dot_general(act_grad, full_weight, (((1,), (1,)), ((), ())), preferre...  28.5 us
    ppermute x14, starting transfers between devices, shifted(): return lax.ppermute(block, axis, route)  18.1 us
  transfers between devices with their start and end apart: 23, of which 16 were waited for; matrix products, arithmetic and copies ran while one was open for 4% of the time, Pallas kernels for 0%

commit v1 on v0

v1 whole, which is shorter than its diff:
```python
import jax
import jax.numpy as jnp
from jax import lax
from jax.sharding import PartitionSpec as P

norm_eps = 1e-06
root_half = 0.7071067811865476
inv_root_two_pi = 0.3989422804014327
lanes = 128


def gelu_parts(pre_act):
    normal_cdf = 0.5 * (1.0 + jax.scipy.special.erf(pre_act * root_half))
    density = jnp.exp(-0.5 * pre_act * pre_act) * inv_root_two_pi
    return (pre_act * normal_cdf, normal_cdf + pre_act * density)


def local_top(llm_grad, slot_row, counts):
    row_count = llm_grad.shape[1]
    slot_ids = jnp.arange(row_count, dtype=jnp.int32)
    kept_mask = slot_ids[None, :] < counts[:, None]
    source = jnp.where(kept_mask[..., None], llm_grad, jnp.zeros_like(llm_grad))
    onehot = (slot_row[:, :, None] == slot_ids[None, None, :]).astype(jnp.bfloat16)
    placed = jnp.einsum("mjr,mjd->mrd", onehot, source, preferred_element_type=jnp.float32)
    return placed.astype(jnp.bfloat16)


def cuts(hidden, parts):
    unit = lanes if hidden % lanes == 0 else 1
    tiles = hidden // unit
    bounds = [tiles * i // parts * unit for i in range(parts + 1)]
    width = max(b - a for a, b in zip(bounds, bounds[1:]))
    return bounds, width


def split_hidden(block, parts):
    bounds, width = cuts(block.shape[-1], parts)
    lead = [(0, 0)] * (block.ndim - 1)
    return jnp.stack(
        [
            jnp.pad(block[..., a:b], lead + [(0, width - (b - a))])
            for a, b in zip(bounds, bounds[1:])
        ]
    )


def merge_hidden(blocks, hidden):
    bounds, width = cuts(hidden, blocks.shape[0])
    return jnp.concatenate(
        [blocks[i][..., : b - a] for i, (a, b) in enumerate(zip(bounds, bounds[1:]))], axis=-1
    )


def exchange(blocks, axes):
    return lax.all_to_all(blocks, axes, 0, 0, tiled=True)


def swap_cores(block):
    return lax.ppermute(block, "tensor", [(0, 1), (1, 0)])


def dot32(left, right, dims):
    return lax.dot_general(left, right, (dims, ((), ())), preferred_element_type=jnp.float32)


def body(llm_grad, slot_row, counts, saved_in, saved_pre, weights, channel_scale):
    sections = lax.axis_size("pipe")
    ranks = lax.axis_size("dp")
    core = lax.axis_index("tensor")
    micro_count, row_count, model_width = llm_grad.shape
    hidden = saved_pre.shape[3]
    tokens = micro_count * row_count
    channels = weights.shape[1]
    columns = sections
    part = tokens // (2 * columns)
    channel_gain = channel_scale[0]

    def all_ranks_rows(rows):
        kinds = rows.shape[0]
        sliced = rows.reshape(kinds, part, ranks, channels).transpose(2, 0, 1, 3)
        sent = jnp.broadcast_to(sliced[:, None], (ranks, columns, kinds, part, channels))
        got = exchange(sent.reshape(ranks * columns, kinds, part, channels), ("dp", "pipe"))
        other = swap_cores(got)
        first = jnp.where(core == 0, got, other)
        second = jnp.where(core == 0, other, got)
        both = jnp.stack([first, second], axis=1)
        return both.transpose(2, 0, 1, 3, 4).reshape(kinds, ranks * tokens, channels)

    def sum_to_rows(partial_sum):
        halves = partial_sum.reshape(ranks * columns, 2, part, channels)
        keep = jnp.where(core == 0, halves[:, 0], halves[:, 1])
        give = jnp.where(core == 0, halves[:, 1], halves[:, 0]).astype(jnp.bfloat16)
        pair = (keep + swap_cores(give).astype(jnp.float32)).astype(jnp.bfloat16)
        got = exchange(pair, ("dp", "pipe")).reshape(ranks, columns, part, channels)
        summed = jnp.sum(got.astype(jnp.float32), axis=1)
        return summed.transpose(1, 0, 2).reshape(part, model_width)

    def sum_over_ranks(partial_sum):
        sent = partial_sum.astype(jnp.bfloat16).reshape(ranks, tokens, -1)
        return jnp.sum(exchange(sent, "dp").astype(jnp.float32), axis=0)

    def all_ranks(block):
        kinds = block.shape[0]
        sent = jnp.broadcast_to(block[None], (ranks,) + block.shape)
        got = exchange(sent, "dp")
        return got.transpose(1, 0, 2, 3).reshape(kinds, ranks * tokens, -1)

    top_grad = local_top(llm_grad, slot_row[:, 0], counts[0])
    top_flat = top_grad.reshape(tokens, model_width)
    scaled_weight = (weights[0].astype(jnp.float32) * channel_gain_rows(channel_gain, channels)).astype(
        jnp.bfloat16
    )
    weight_parts = exchange(split_hidden(scaled_weight, columns), "pipe")
    top_sliced = top_flat.reshape(tokens, ranks, channels).transpose(1, 0, 2)
    grad_all = exchange(top_sliced, "dp").reshape(ranks * tokens, channels)
    pre_parts = exchange(split_hidden(saved_pre[0].reshape(tokens, hidden), columns), "pipe")
    in_halves = saved_in[0].reshape(columns, 2, part, model_width)
    in_half = jnp.where(core == 0, in_halves[:, 0], in_halves[:, 1])
    in_parts = exchange(in_half, "pipe")

    def gain_free_norm(values):
        values = values.astype(jnp.float32)
        center = values - jnp.mean(values, axis=-1, keepdims=True)
        inv_std = lax.rsqrt(jnp.mean(center * center, axis=-1, keepdims=True) + norm_eps)
        return center * inv_std, inv_std

    ups = list(range(sections - 2, -1, -2))
    downs = list(range(sections - 1, -1, -2))
    units = {}
    for s in ups:
        units[s] = gain_free_norm(in_parts[s])
    unit_all = all_ranks_rows(jnp.stack([units[s][0].astype(jnp.bfloat16) for s in ups]))
    activated = jnp.stack(
        [gelu_parts(pre_parts[s].astype(jnp.float32))[0].astype(jnp.bfloat16) for s in downs]
    )
    activated_all = all_ranks(activated)

    top_halves = top_flat.reshape(columns, 2, part, model_width)
    column = lax.axis_index("pipe")
    own = lax.dynamic_index_in_dim(top_halves, column, 0, keepdims=False)
    incoming = jnp.where(core == 0, own[0], own[1])
    weight_grads = [None] * sections
    outgoing = [None] * sections
    for pair, (up, down) in enumerate(zip(ups, downs)):
        partial_hidden = dot32(grad_all, weight_parts[down], ((1,), (0,)))
        hidden_grad = sum_over_ranks(partial_hidden)
        slope = gelu_parts(pre_parts[up].astype(jnp.float32))[1]
        act_grad = all_ranks((hidden_grad * slope).astype(jnp.bfloat16)[None])[0]
        back = sum_to_rows(dot32(act_grad, weight_parts[up], ((1,), (1,))))
        unit, inv_std = units[up]
        back = inv_std * (
            back
            - jnp.mean(back, axis=-1, keepdims=True)
            - unit * jnp.mean(back * unit, axis=-1, keepdims=True)
        )
        weight_grads[down] = dot32(grad_all, activated_all[pair], ((0,), (0,)))
        weight_grads[up] = dot32(unit_all[pair], act_grad, ((0,), (0,)))
        outgoing[down] = incoming
        incoming = (incoming.astype(jnp.float32) + back).astype(jnp.bfloat16)
        outgoing[up] = incoming
        if up > 0:
            grad_all = all_ranks_rows(incoming[None])[0]

    returned = exchange(jnp.stack(weight_grads).astype(jnp.bfloat16), "pipe")
    merged = merge_hidden(returned, hidden).astype(jnp.float32)
    weight_out = (merged * channel_gain_rows(channel_gain, channels)).astype(jnp.bfloat16)

    sent_rows = exchange(jnp.stack(outgoing), "pipe")
    other_rows = swap_cores(sent_rows)
    first = jnp.where(core == 0, sent_rows, other_rows)
    second = jnp.where(core == 0, other_rows, sent_rows)
    section_out = jnp.stack([first, second], axis=1).reshape(micro_count, row_count, model_width)
    return (weight_out[None], section_out[None])


def channel_gain_rows(channel_gain, channels):
    start = lax.axis_index("dp") * channels
    return lax.dynamic_slice_in_dim(channel_gain, start, channels, 0)[:, None]


def solution(mesh):
    in_specs = (
        P(None, "dp", None),
        P(None, "dp", None),
        P("dp", None),
        P("pipe", None, "dp", None),
        P("pipe", None, "dp", "tensor"),
        P("pipe", "dp", "tensor"),
        P("pipe", None),
    )
    out_specs = (P("pipe", "dp", "tensor"), P("pipe", None, "dp", None))
    return jax.shard_map(body, mesh=mesh, in_specs=in_specs, out_specs=out_specs, check_vma=False)
```

time: 670 us -> 366 us (0.55)
  waiting for transfers between devices: 538 us -> 171 us
  blocking collectives: 0 us -> 102 us
  matrix products: 37.9 us -> 12.8 us
  starting transfers between devices: 18.2 us -> 42.5 us
  other arithmetic: 32.5 us -> 19.3 us
  between operations: 13.8 us -> 1.3 us
  local copies, waits for them, and re-layouts: 22 us -> 15.1 us
    all_gather x1 -> x0, waiting for transfers between devices: 189 us -> none  [body(): full_weight = lax.all_gather(weights[0], 'dp', axis=0, tiled=True)]
    reduce_scatter x1 -> x0, waiting for transfers between devices: 182 us -> none  [body(): lax.psum_scatter(lax.dot_general(flat_left, flat_right, (((0,), (0,)), ((...]
    all_to_all x0 -> x11, waiting for transfers between devices: none -> 167 us  [exchange(): return lax.all_to_all(blocks, axes, 0, 0, tiled=True)]
    psum x7 -> x0, waiting for transfers between devices: 131 us -> none  [advance(): lax.psum(shortened(partial_value), 'tensor')]
    all_to_all x0 -> x4, blocking collectives: none -> 102 us  [exchange(): return lax.all_to_all(blocks, axes, 0, 0, tiled=True)]
    all_to_all x0 -> x11, starting transfers between devices: none -> 42.3 us  [exchange(): return lax.all_to_all(blocks, axes, 0, 0, tiled=True)]
    ppermute x14 -> x5, waiting for transfers between devices: 36.1 us -> 4.51 us  [swap_cores(): return lax.ppermute(block, 'tensor', [(0, 1), (1, 0)])]
    dot_general x5 -> x8, matrix products: 36.5 us -> 11.5 us  [dot32(): lax.dot_general(left, right, (dims, ((), ())), preferred_element_type=jnp...]
  transfers between devices with their start and end apart: 23 -> 16, of which waited for: 16 -> 14; matrix products, arithmetic and copies ran while one was open for 4% -> 6% of each run, Pallas kernels for 0% -> 0%
where the time goes in v1:
time: 366 us; the launch traced here: 364 us
  waiting for transfers between devices  171 us (47%)
  blocking collectives  102 us (28%)
  starting transfers between devices  42.5 us (12%)
  other arithmetic  19.3 us (5%)
  local copies, waits for them, and re-layouts  15.1 us (4%)
  matrix products  12.8 us (3%)
    all_to_all x11, waiting for transfers between devices, exchange(): return lax.all_to_all(blocks, axes, 0, 0, tiled=True)  167 us
    all_to_all x4, blocking collectives, exchange(): return lax.all_to_all(blocks, axes, 0, 0, tiled=True)  102 us
    all_to_all x11, starting transfers between devices, exchange(): return lax.all_to_all(blocks, axes, 0, 0, tiled=True)  42.3 us
    dot_general x8, matrix products, dot32(): lax.dot_general(left, right, (dims, ((), ())), preferred_element_type=jnp...  11.5 us
  transfers between devices with their start and end apart: 16, of which 14 were waited for; matrix products, arithmetic and copies ran while one was open for 6% of the time, Pallas kernels for 0%

profile of v1, /device:TPU:0, one launch (start us, length us, event | category | flops | bytes accessed | tf_op | source)
XLA Modules:
  0.0 363.9 jit_solution(15783915915604211753)
XLA Ops:
  4.4 2.2 copy.74
  6.6 6.3 %all-to-all-start.2 = ((bf16[4,128,416]{1,2,0:T(8,128)(2,1)}), bf16[4,128,416]{1,2,0:T(8,128)(2,1)}, u32[]{:S(2)}, u32[]{:S(2)}) async-start(bf16[4,128,416]{1,2,0:T(8,128)(2,1)} %copy.74), calls=%async_computation.2 | async-start | bytes 851968 | tf_op jit(solution)/shard_map/all_to_all | solution.py:55
  15.1 10.4 %all-to-all-done.2 = bf16[4,128,416]{1,2,0:T(8,128)(2,1)} async-done(((bf16[4,128,416]{1,2,0:T(8,128)(2,1)}), bf16[4,128,416]{1,2,0:T(8,128)(2,1)}, u32[]{:S(2)}, u32[]{:S(2)}) %all-to-all-start.2) | async-done | bytes 426016 | tf_op jit(solution)/shard_map/all_to_all | solution.py:55
  25.5 37.7 %all_to_all.75 = bf16[4,416,896]{2,1,0:T(8,128)(2,1)S(1)} all-to-all(bf16[4,416,896]{2,1,0:T(8,128)(2,1)S(1)} %pad_maximum_fusion), channel_id=1, replica_groups=mesh['pipe'=4,'dp'=4,'tensor'=2] {'pipe'}, dimensions={0} | all-to-all | bytes 5963776 | tf_op jit(solution)/shard_map/all_to_all | solution.py:55
  64.8 2.8 convolution_convert_fusion.2
  67.6 3.5 all-to-all-start.4
  72.3 19.8 %all-to-all-done.4 = bf16[4,128,896]{2,1,0:T(8,128)(2,1)S(1)} async-done(((bf16[4,128,896]{2,1,0:T(8,128)(2,1)}), bf16[4,128,896]{2,1,0:T(8,128)(2,1)S(1)}, u32[]{:S(2)}, u32[]{:S(2)}) %all-to-all-start.4) | async-done | bytes 917536 | tf_op jit(solution)/shard_map/all_to_all | solution.py:55
  92.1 3.5 all-to-all-start.5
  95.8 11.6 %all-to-all-done.5 = bf16[4,128,896]{2,1,0:T(8,128)(2,1)S(1)} async-done(((bf16[4,128,896]{2,1,0:T(8,128)(2,1)}), bf16[4,128,896]{2,1,0:T(8,128)(2,1)S(1)}, u32[]{:S(2)}, u32[]{:S(2)}) %all-to-all-start.5) | async-done | bytes 917536 | tf_op jit(solution)/shard_map/all_to_all | solution.py:55
  108.6 3.5 all-to-all-start.6
  113.1 21.5 %all-to-all-done.6 = bf16[4,1,128,896]{3,2,1,0:T(8,128)(2,1)S(1)} async-done(((bf16[4,1,128,896]{3,2,1,0:T(8,128)(2,1)}), bf16[4,1,128,896]{3,2,1,0:T(8,128)(2,1)S(1)}, u32[]{:S(2)}, u32[]{:S(2)}) %all-to-all-start.6) | async-done | bytes 917536 | tf_op jit(solution)/shard_map/all_to_all | solution.py:55
  134.5 4.0 %all-to-all-start = ((bf16[4,16,1664]{2,1,0:T(8,128)(2,1)}), bf16[4,16,1664]{2,1,0:T(8,128)(2,1)}, u32[]{:S(2)}, u32[]{:S(2)}) async-start(bf16[4,16,1664]{2,1,0:T(8,128)(2,1)} %fusion.46), calls=%async_computation | async-start | bytes 425984 | tf_op jit(solution)/shard_map/all_to_all | solution.py:55
  138.5 1.8 fusion.7
  141.1 2.7 all-to-all-done
  146.3 1.8 fusion.11
  148.1 3.5 all-to-all-start.7
  153.8 7.3 %all-to-all-done.7 = bf16[16,16,416]{2,1,0:T(8,128)(2,1)S(1)} async-done(((bf16[16,16,416]{2,1,0:T(8,128)(2,1)}), bf16[16,16,416]{2,1,0:T(8,128)(2,1)S(1)}, u32[]{:S(2)}, u32[]{:S(2)}) %all-to-all-start.7) | async-done | bytes 213024 | tf_op jit(solution)/shard_map/all_to_all | solution.py:55
  161.7 12.7 %all_to_all.76 = bf16[16,1,16,416]{3,2,1,0:T(8,128)(2,1)S(1)} all-to-all(bf16[16,1,16,416]{3,2,1,0:T(8,128)(2,1)S(1)} %bitcast.210), channel_id=1, replica_groups=mesh['pipe'=4,'dp'=4,'tensor'=2] {'dp','pipe'}, dimensions={0} | all-to-all | bytes 425984 | tf_op jit(solution)/shard_map/all_to_all | solution.py:55
  176.9 26.1 %all_to_all.77 = bf16[4,128,896]{2,1,0:T(8,128)(2,1)S(1)} all-to-all(bf16[4,128,896]{2,1,0:T(8,128)(2,1)S(1)} %bitcast.213), channel_id=1, replica_groups=mesh['pipe'=4,'dp'=4,'tensor'=2] {'dp'}, dimensions={0} | all-to-all | bytes 1835008 | tf_op jit(solution)/shard_map/all_to_all | solution.py:55
  203.4 25.0 %all_to_all.78 = bf16[4,1,128,896]{3,2,1,0:T(8,128)(2,1)S(1)} all-to-all(bf16[4,1,128,896]{3,2,1,0:T(8,128)(2,1)S(1)} %broadcast_in_dim.31), channel_id=1, replica_groups=mesh['pipe'=4,'dp'=4,'tensor'=2] {'dp'}, dimensions={0} | all-to-all | bytes 1835008 | tf_op jit(solution)/shard_map/all_to_all | solution.py:55
  232.6 3.5 all-to-all-start.13
  236.4 10.1 %all-to-all-done.13 = bf16[16,16,416]{2,1,0:T(8,128)(2,1)S(1)} async-done(((bf16[16,16,416]{2,1,0:T(8,128)(2,1)}), bf16[16,16,416]{2,1,0:T(8,128)(2,1)S(1)}, u32[]{:S(2)}, u32[]{:S(2)}) %all-to-all-start.13) | async-done | bytes 213024 | tf_op jit(solution)/shard_map/all_to_all | solution.py:55
  248.0 3.6 all-to-all-start.11
  254.7 38.4 %all-to-all-done.11 = bf16[4,2,128,896]{3,2,1,0:T(8,128)(2,1)S(1)} async-done(((bf16[4,2,128,896]{3,2,1,0:T(8,128)(2,1)}), bf16[4,2,128,896]{3,2,1,0:T(8,128)(2,1)S(1)}, u32[]{:S(2)}, u32[]{:S(2)}) %all-to-all-start.11) | async-done | bytes 1835040 | tf_op jit(solution)/shard_map/all_to_all | solution.py:55
  294.0 3.8 %all-to-all-start.1 = ((bf16[16,2,16,416]{3,2,1,0:T(8,128)(2,1)}), bf16[16,2,16,416]{3,2,1,0:T(8,128)(2,1)S(1)}, u32[]{:S(2)}, u32[]{:S(2)}) async-start(bf16[16,2,16,416]{3,2,1,0:T(8,128)(2,1)} %bitcast.5), calls=%async_computation.1 | async-start | bytes 1048576 | tf_op jit(solution)/shard_map/all_to_all | solution.py:55
  297.9 2.5 fusion.4
  300.4 11.7 %all-to-all-done.1 = bf16[16,2,16,416]{3,2,1,0:T(8,128)(2,1)S(1)} async-done(((bf16[16,2,16,416]{3,2,1,0:T(8,128)(2,1)}), bf16[16,2,16,416]{3,2,1,0:T(8,128)(2,1)S(1)}, u32[]{:S(2)}, u32[]{:S(2)}) %all-to-all-start.1) | async-done | bytes 426016 | tf_op jit(solution)/shard_map/all_to_all | solution.py:55
  314.6 3.4 all-to-all-start.14
  320.5 1.8 pad_maximum_fusion.1
  323.7 3.7 %all-to-all-start.12 = ((bf16[4,416,896]{2,1,0:T(8,128)(2,1)}), bf16[4,416,896]{2,1,0:T(8,128)(2,1)S(1)}, u32[]{:S(2)}, u32[]{:S(2)}) async-start(bf16[4,416,896]{2,1,0:T(8,128)(2,1)} %pad_maximum_fusion.1), calls=%async_computation.12 | async-start | bytes 5963776 | tf_op jit(solution)/shard_map/all_to_all | solution.py:55
  329.9 31.8 %all-to-all-done.12 = bf16[4,416,896]{2,1,0:T(8,128)(2,1)S(1)} async-done(((bf16[4,416,896]{2,1,0:T(8,128)(2,1)}), bf16[4,416,896]{2,1,0:T(8,128)(2,1)S(1)}, u32[]{:S(2)}, u32[]{:S(2)}) %all-to-all-start.12) | async-done | bytes 2981920 | tf_op jit(solution)/shard_map/all_to_all | solution.py:55
  362.0 1.8 multiply_convert_fusion
  (123 shorter events, 38.5 us)
Async XLA Ops:
  0.6 12.3 %copy-start = (f32[1,1664]{1,0:T(1,128)S(1)}, f32[1,1664]{1,0:T(1,128)}, u32[]{:S(2)}) copy-start(f32[1,1664]{1,0:T(1,128)} %param.13) | copy-start | bytes 19972
  0.6 12.4 %copy-start.8 = (bf16[1,416,3200]{2,1,0:T(8,128)(2,1)S(1)}, bf16[1,416,3200]{2,1,0:T(8,128)(2,1)}, u32[]{:S(2)}) copy-start(bf16[1,416,3200]{2,1,0:T(8,128)(2,1)} %param.12) | copy-start | bytes 7987204
  6.6 18.8 %all-to-all-start.2 = ((bf16[4,128,416]{1,2,0:T(8,128)(2,1)}), bf16[4,128,416]{1,2,0:T(8,128)(2,1)}, u32[]{:S(2)}, u32[]{:S(2)}) async-start(bf16[4,128,416]{1,2,0:T(8,128)(2,1)} %copy.74), calls=%async_computation.2 | async-start | bytes 851968 | tf_op jit(solution)/shard_map/all_to_all | solution.py:55
  13.8 0.7 copy-start.15
  63.2 1.6 copy-start.6
  64.8 6.3 %copy-start.10 = (bf16[1,4,32,3200]{3,2,1,0:T(8,128)(2,1)S(1)}, bf16[1,4,32,3200]{3,2,1,0:T(8,128)(2,1)}, u32[]{:S(2)}) copy-start(bf16[1,4,32,3200]{3,2,1,0:T(8,128)(2,1)} %param.11) | copy-start | bytes 2457604
  67.6 24.6 %all-to-all-start.4 = ((bf16[4,128,896]{2,1,0:T(8,128)(2,1)}), bf16[4,128,896]{2,1,0:T(8,128)(2,1)S(1)}, u32[]{:S(2)}, u32[]{:S(2)}) async-start(bf16[4,128,896]{2,1,0:T(8,128)(2,1)} %bitcast.21), calls=%async_computation.4 | async-start | bytes 1835008 | tf_op jit(solution)/shard_map/all_to_all | solution.py:55
  92.1 15.3 %all-to-all-start.5 = ((bf16[4,128,896]{2,1,0:T(8,128)(2,1)}), bf16[4,128,896]{2,1,0:T(8,128)(2,1)S(1)}, u32[]{:S(2)}, u32[]{:S(2)}) async-start(bf16[4,128,896]{2,1,0:T(8,128)(2,1)} %pad_maximum_fusion.2), calls=%async_computation.5 | async-start | bytes 1835008 | tf_op jit(solution)/shard_map/all_to_all | solution.py:55
  95.6 16.7 %copy-start.13 = (bf16[1,4,32,1664]{3,2,1,0:T(8,128)(2,1)S(1)}, bf16[1,4,32,1664]{3,2,1,0:T(8,128)(2,1)}, u32[]{:S(2)}) copy-start(bf16[1,4,32,1664]{3,2,1,0:T(8,128)(2,1)} %param.10) | copy-start | bytes 1277956
  108.6 25.9 %all-to-all-start.6 = ((bf16[4,1,128,896]{3,2,1,0:T(8,128)(2,1)}), bf16[4,1,128,896]{3,2,1,0:T(8,128)(2,1)S(1)}, u32[]{:S(2)}, u32[]{:S(2)}) async-start(bf16[4,1,128,896]{3,2,1,0:T(8,128)(2,1)} %broadcast_in_dim.27), calls=%async_computation.6 | async-start | bytes 1835008 | tf_op jit(solution)/shard_map/all_to_all | solution.py:55
  134.5 13.6 %copy-start.2 = (bf16[4,1,128,896]{3,2,1,0:T(8,128)(2,1)}, bf16[4,1,128,896]{3,2,1,0:T(8,128)(2,1)S(1)}, u32[]{:S(2)}) copy-start(bf16[4,1,128,896]{3,2,1,0:T(8,128)(2,1)S(1)} %all-to-all-done.6) | copy-start | bytes 2752516
  134.5 9.3 %all-to-all-start = ((bf16[4,16,1664]{2,1,0:T(8,128)(2,1)}), bf16[4,16,1664]{2,1,0:T(8,128)(2,1)}, u32[]{:S(2)}, u32[]{:S(2)}) async-start(bf16[4,16,1664]{2,1,0:T(8,128)(2,1)} %fusion.46), calls=%async_computation | async-start | bytes 425984 | tf_op jit(solution)/shard_map/all_to_all | solution.py:55
  141.1 5.2 %collective-permute-start.1 = (bf16[16,16,416]{2,1,0:T(8,128)(2,1)}, bf16[16,16,416]{2,1,0:T(8,128)(2,1)}, u32[]{:S(2)}, u32[]{:S(2)}) collective-permute-start(bf16[16,16,416]{2,1,0:T(8,128)(2,1)} %fusion.43), channel_id=1, source_target_pairs={{0,1},{1,0},{2,3},{3,2},{4,5},{5,4},{6,7},{7,6},{8,9},{9,8},{10,11... | collective-permute-start | bytes 638984 | tf_op jit(solution)/shard_map/ppermute | solution.py:59
  148.1 13.0 %all-to-all-start.7 = ((bf16[16,16,416]{2,1,0:T(8,128)(2,1)}), bf16[16,16,416]{2,1,0:T(8,128)(2,1)S(1)}, u32[]{:S(2)}, u32[]{:S(2)}) async-start(bf16[16,16,416]{2,1,0:T(8,128)(2,1)} %fusion.11), calls=%async_computation.7 | async-start | bytes 524288 | tf_op jit(solution)/shard_map/all_to_all | solution.py:55
  161.1 15.0 %copy-start.7 = (bf16[4,416,896]{2,1,0:T(8,128)(2,1)S(1)}, bf16[4,416,896]{2,1,0:T(8,128)(2,1)}, u32[]{:S(2)}) copy-start(bf16[4,416,896]{2,1,0:T(8,128)(2,1)} %copy-done.6) | copy-start | bytes 8945668
  174.5 1.5 collective-permute-start.2
  176.2 27.2 %copy-start.9 = (bf16[16,2,1,16,416]{4,3,1,0,2:T(8,128)(2,1)}, bf16[16,2,1,16,416]{4,3,1,0,2:T(8,128)(2,1)S(1)}, u32[]{:S(2)}) copy-start(bf16[16,2,1,16,416]{4,3,1,0,2:T(8,128)(2,1)S(1)} %copy.85) | copy-start | bytes 1277956
  228.4 0.9 copy-start.4
  230.2 1.6 collective-permute-start.3
  232.6 13.9 %all-to-all-start.13 = ((bf16[16,16,416]{2,1,0:T(8,128)(2,1)}), bf16[16,16,416]{2,1,0:T(8,128)(2,1)S(1)}, u32[]{:S(2)}, u32[]{:S(2)}) async-start(bf16[16,16,416]{2,1,0:T(8,128)(2,1)} %fusion.12), calls=%async_computation.13 | async-start | bytes 524288 | tf_op jit(solution)/shard_map/all_to_all | solution.py:55
  236.4 15.2 %copy-start.12 = (f32[1,16,1664]{2,1,0:T(8,128)S(1)}, f32[1,16,1664]{2,1,0:T(8,128)}, u32[]{:S(2)}) copy-start(f32[1,16,1664]{2,1,0:T(8,128)} %get-tuple-element.35) | copy-start | bytes 319492
  248.0 45.1 %all-to-all-start.11 = ((bf16[4,2,128,896]{3,2,1,0:T(8,128)(2,1)}), bf16[4,2,128,896]{3,2,1,0:T(8,128)(2,1)S(1)}, u32[]{:S(2)}, u32[]{:S(2)}) async-start(bf16[4,2,128,896]{3,2,1,0:T(8,128)(2,1)} %broadcast_in_dim.32), calls=%async_computation.11 | async-start | bytes 3670016 | tf_op jit(solution)/shard_map/all_to_all | solution.py:55
  294.0 18.2 %all-to-all-start.1 = ((bf16[16,2,16,416]{3,2,1,0:T(8,128)(2,1)}), bf16[16,2,16,416]{3,2,1,0:T(8,128)(2,1)S(1)}, u32[]{:S(2)}, u32[]{:S(2)}) async-start(bf16[16,2,16,416]{3,2,1,0:T(8,128)(2,1)} %bitcast.5), calls=%async_computation.1 | async-start | bytes 1048576 | tf_op jit(solution)/shard_map/all_to_all | solution.py:55
  297.9 15.9 %copy-start.14 = (bf16[1,16,1664]{2,1,0:T(8,128)(2,1)S(1)}, bf16[1,16,1664]{2,1,0:T(8,128)(2,1)}, u32[]{:S(2)}) copy-start(bf16[1,16,1664]{2,1,0:T(8,128)(2,1)} %get-tuple-element.8) | copy-start | bytes 159748
  312.2 5.8 %collective-permute-start = (bf16[16,2,16,416]{3,2,1,0:T(8,128)(2,1)S(1)}, bf16[16,2,16,416]{3,2,1,0:T(8,128)(2,1)S(1)}, u32[]{:S(2)}, u32[]{:S(2)}) collective-permute-start(bf16[16,2,16,416]{3,2,1,0:T(8,128)(2,1)S(1)} %all-to-all-done.1), channel_id=1, source_target_pairs={{0,1},{1,0},{2,3},{3,2},{4,5},{5,4},{6,7},{7,6},{8,9},{9,8},{10,11... | collective-permute-start | bytes 1277960 | tf_op jit(solution)/shard_map/ppermute | solution.py:59
  314.6 9.2 %all-to-all-start.14 = ((bf16[4,16,1664]{2,1,0:T(8,128)(2,1)}), bf16[4,16,1664]{2,1,0:T(8,128)(2,1)S(1)}, u32[]{:S(2)}, u32[]{:S(2)}) async-start(bf16[4,16,1664]{2,1,0:T(8,128)(2,1)} %pad_maximum_fusion.6), calls=%async_computation.14 | async-start | bytes 425984 | tf_op jit(solution)/shard_map/all_to_all | solution.py:55
  318.0 1.2 copy-start.5
  318.2 1.7 copy-start.3
  318.3 2.2 copy-start.11
  323.7 37.9 %all-to-all-start.12 = ((bf16[4,416,896]{2,1,0:T(8,128)(2,1)}), bf16[4,416,896]{2,1,0:T(8,128)(2,1)S(1)}, u32[]{:S(2)}, u32[]{:S(2)}) async-start(bf16[4,416,896]{2,1,0:T(8,128)(2,1)} %pad_maximum_fusion.1), calls=%async_computation.12 | async-start | bytes 5963776 | tf_op jit(solution)/shard_map/all_to_all | solution.py:55
  327.4 1.5 collective-permute-start.4
  362.0 1.9 copy-start.1

commit v2 on v1

v2 whole, which is shorter than its diff:
```python
import jax
import jax.numpy as jnp
from jax import lax
from jax.sharding import PartitionSpec as P

norm_eps = 1e-06
root_half = 0.7071067811865476
inv_root_two_pi = 0.3989422804014327
lanes = 128
aside_limit = 8


def gelu_parts(pre_act):
    normal_cdf = 0.5 * (1.0 + jax.scipy.special.erf(pre_act * root_half))
    density = jnp.exp(-0.5 * pre_act * pre_act) * inv_root_two_pi
    return (pre_act * normal_cdf, normal_cdf + pre_act * density)


def local_top(llm_grad, slot_row, counts):
    row_count = llm_grad.shape[1]
    slot_ids = jnp.arange(row_count, dtype=jnp.int32)
    kept_mask = slot_ids[None, :] < counts[:, None]
    source = jnp.where(kept_mask[..., None], llm_grad, jnp.zeros_like(llm_grad))
    onehot = (slot_row[:, :, None] == slot_ids[None, None, :]).astype(jnp.bfloat16)
    placed = jnp.einsum("mjr,mjd->mrd", onehot, source, preferred_element_type=jnp.float32)
    return placed.astype(jnp.bfloat16)


def cuts(hidden, parts):
    unit = lanes if hidden % lanes == 0 else 1
    tiles = hidden // unit
    bounds = [tiles * i // parts * unit for i in range(parts + 1)]
    width = max(b - a for a, b in zip(bounds, bounds[1:]))
    starts = [min(a, hidden - width) for a in bounds[:-1]]
    fresh = [b - a for a, b in zip(starts, starts[1:] + [hidden])]
    return starts, fresh, width


def lookup(values, index):
    found = jnp.int32(values[-1])
    for i, value in enumerate(values[:-1]):
        found = jnp.where(index == i, jnp.int32(value), found)
    return found


def exchange(blocks, axes):
    return lax.all_to_all(blocks, axes, 0, 0, tiled=True)


def swap_cores(block):
    return lax.ppermute(block, "tensor", [(0, 1), (1, 0)])


def dot32(left, right, dims):
    return lax.dot_general(left, right, (dims, ((), ())), preferred_element_type=jnp.float32)


def channel_gain_rows(channel_gain, channels):
    start = lax.axis_index("dp") * channels
    return lax.dynamic_slice_in_dim(channel_gain, start, channels, 0)[:, None]


def partner(index, distance, count):
    assert count & (count - 1) == 0
    return index ^ distance


def swap_columns(block, distance, keep=None):
    count = lax.axis_size("pipe")
    route = [(i, partner(i, distance, count)) for i in range(count)]
    route = [pair for pair in route if keep is None or keep(*pair)]
    return lax.ppermute(block, "pipe", route)


def choose(which, blocks):
    return lax.select_n(which, *blocks)


def after(block, *others):
    return lax.optimization_barrier((block,) + others)[0]


def exact_halves(values):
    high = lax.reduce_precision(values, 8, 7)
    return high.astype(jnp.bfloat16), (values - high).astype(jnp.bfloat16)


def centred_unit(values):
    values = values.astype(jnp.float32)
    center = values - jnp.mean(values, axis=-1, keepdims=True)
    inv_std = lax.rsqrt(jnp.mean(center * center, axis=-1, keepdims=True) + norm_eps)
    return center * inv_std, inv_std


def layer(llm_grad, slot_row, counts, saved_in, saved_pre, weights, channel_scale):
    sections = columns = lax.axis_size("pipe")
    ranks = lax.axis_size("dp")
    core = lax.axis_index("tensor")
    column = lax.axis_index("pipe")
    rank = lax.axis_index("dp")
    micro_count, row_count, model_width = llm_grad.shape
    hidden = saved_pre.shape[3]
    tokens = micro_count * row_count
    all_tokens = ranks * tokens
    channels = weights.shape[1]
    part = tokens // (2 * columns)
    piece = channels // columns
    starts, fresh, width = cuts(hidden, columns)
    gain_rows = channel_gain_rows(channel_scale[0], channels)
    ups = list(range(sections - 2, -1, -2))
    downs = list(range(sections - 1, -1, -2))
    own_fresh = lookup(fresh, column)
    is_fresh = lax.broadcasted_iota(jnp.int32, (1, width), 1) < own_fresh

    def mine(halves):
        return jnp.where(core == 0, halves[0], halves[1])

    def theirs(halves):
        return jnp.where(core == 0, halves[1], halves[0])

    def both_cores(block, axis):
        other = swap_cores(block)
        first = jnp.where(core == 0, block, other)
        second = jnp.where(core == 0, other, block)
        return jnp.stack([first, second], axis=axis)

    def hidden_piece(block, to):
        return lax.dynamic_slice_in_dim(block, lookup(starts, to), width, block.ndim - 1)

    def by_section(got):
        return [choose(partner(column, s, columns), got) for s in range(sections)]

    def scatter_hidden(block, ready=lambda piece: piece):
        pieces = [ready(hidden_piece(block, partner(column, d, columns))) for d in range(columns)]
        return [pieces[0]] + [swap_columns(pieces[d], d) for d in range(1, columns)]

    def token_halves(block):
        halves = block.reshape(ranks * columns, 2, part, channels)
        return halves[:, 0], halves[:, 1]

    def sum_to_rows(partial_sum, whole):
        halves = token_halves(partial_sum)
        given = theirs(halves).astype(jnp.bfloat16)
        pair = (mine(halves) + swap_cores(given).astype(jnp.float32)).astype(jnp.bfloat16)
        share = lax.dynamic_slice_in_dim(mine(token_halves(whole)), column * piece, piece, 2)
        got = exchange(jnp.concatenate([pair, share], axis=-1), ("dp", "pipe"))
        got = got.reshape(ranks, columns, part, channels + piece)
        summed = jnp.sum(got[..., :channels].astype(jnp.float32), axis=1)
        summed = summed.transpose(1, 0, 2).reshape(part, model_width)
        return summed, got[..., channels:].transpose(2, 0, 1, 3).reshape(part, model_width)

    def sum_over_ranks(partial_sum):
        sent = partial_sum.astype(jnp.bfloat16).reshape(ranks, tokens, -1)
        return jnp.sum(exchange(sent, "dp").astype(jnp.float32), axis=0)

    def all_ranks(block):
        sent = jnp.broadcast_to(block[None], (ranks,) + block.shape)
        return exchange(sent, "dp").reshape(all_tokens, -1)

    def all_ranks_aside(block):
        if ranks > aside_limit:
            sent = jnp.broadcast_to(block[None], (ranks,) + block.shape)
            return exchange(sent, "dp").reshape((all_tokens,) + block.shape[1:])
        got = [block]
        for distance in range(1, ranks):
            route = [(i, (i + distance) % ranks) for i in range(ranks)]
            got.append(lax.ppermute(block, "dp", route))
        return got

    def turned(block):
        by_rank = block.reshape(ranks, tokens, -1)
        if ranks > aside_limit:
            return block
        order = [
            lax.dynamic_index_in_dim(by_rank, (rank + ranks - d) % ranks, 0, keepdims=False)
            for d in range(ranks)
        ]
        return jnp.concatenate(order, axis=0)

    def to_channels(rows):
        return exchange(rows.transpose(1, 0, 2), "dp").reshape(all_tokens, -1)

    weight_got = scatter_hidden(
        weights[0], lambda block: (block.astype(jnp.float32) * gain_rows).astype(jnp.bfloat16)
    )
    top_rows = local_top(llm_grad, slot_row[:, 0], counts[0]).reshape(tokens, model_width)
    grad_all = to_channels(top_rows.reshape(tokens, ranks, channels))

    own_in = saved_in[0].reshape(tokens, model_width)
    own_unit, own_std = centred_unit(own_in)
    std_terms = jnp.stack(exact_halves(own_std), axis=-1)
    unit_sent = jnp.concatenate(
        [
            own_unit.astype(jnp.bfloat16).reshape(tokens, ranks, channels),
            jnp.broadcast_to(std_terms, (tokens, ranks, 2)),
        ],
        axis=-1,
    )
    unit_half = mine(to_channels(unit_sent).reshape(2, all_tokens // 2, channels + 2))
    grad_all = after(grad_all, unit_half)

    pre_flat = after(saved_pre[0].reshape(tokens, hidden), *weight_got)
    pre_parts = by_section(scatter_hidden(pre_flat))
    weight_parts = by_section(weight_got)
    unit_half = after(unit_half, *pre_parts)
    unit_got = [unit_half] + [
        swap_columns(unit_half, d, lambda a, b: a % 2 == 0) for d in range(1, columns)
    ]
    units = {s: both_cores(choose(partner(column, s, columns), unit_got), 0) for s in ups}
    units = {s: unit.reshape(all_tokens, channels + 2) for s, unit in units.items()}
    in_halves = own_in.reshape(columns, 2, part, model_width)
    in_halves = jnp.where(core == 0, in_halves[:, 0], in_halves[:, 1])
    in_got = [lax.dynamic_index_in_dim(in_halves, column, 0, keepdims=False)]
    for d in range(1, columns):
        to = partner(column, d, columns)
        sent = lax.dynamic_index_in_dim(in_halves, to, 0, keepdims=False)
        in_got.append(swap_columns(sent, d, lambda a, b: a == 0))
    last_in = choose(column, in_got)

    def hidden_chain(down, up, grad):
        partial_hidden = dot32(grad, weight_parts[down], ((1,), (0,)))
        slope = gelu_parts(pre_parts[up].astype(jnp.float32))[1]
        slope = lax.optimization_barrier(slope)
        return (sum_over_ranks(partial_hidden) * slope).astype(jnp.bfloat16)

    def input_grad(up, act_grad):
        fresh_weight = jnp.where(is_fresh, weight_parts[up], jnp.zeros_like(weight_parts[up]))
        return dot32(act_grad, fresh_weight, ((1,), (1,)))

    def norm_back(incoming, back, unit, inv_std, mean_back, mean_both):
        back = inv_std * (back - mean_back - unit * mean_both)
        return (incoming.astype(jnp.float32) + back).astype(jnp.bfloat16)

    def activated(s):
        return gelu_parts(pre_parts[s].astype(jnp.float32))[0].astype(jnp.bfloat16)

    sides = [None] * sections
    grads = {downs[0]: grad_all}
    for up, down in zip(ups[:-1], downs):
        act_grad = all_ranks(hidden_chain(down, up, grad_all))
        sides[up] = (units[up][:, :channels], act_grad)
        back = input_grad(up, act_grad)
        unit = units[up][:, :channels].astype(jnp.float32)
        sums = jnp.stack([jnp.sum(back, axis=1), jnp.sum(back * unit, axis=1)])
        sums = sums.reshape(2 * all_tokens // lanes, lanes)
        devices = ranks * columns * 2
        sums = exchange(
            jnp.broadcast_to(sums[None], (devices,) + sums.shape), ("dp", "pipe", "tensor")
        )
        sums = (jnp.sum(sums, axis=0) / model_width).reshape(2, all_tokens)
        halves = back.reshape(2, all_tokens // 2, channels)
        pair = mine(halves) + swap_cores(theirs(halves).astype(jnp.bfloat16)).astype(jnp.float32)
        pair = pair.astype(jnp.bfloat16)
        summed = pair.astype(jnp.float32)
        for d in range(1, columns):
            summed = summed + swap_columns(pair, d).astype(jnp.float32)
        own_unit_half = mine(units[up].reshape(2, all_tokens // 2, channels + 2)).astype(jnp.float32)
        own_sums = mine(sums.reshape(2, 2, all_tokens // 2).transpose(1, 0, 2))
        new_half = norm_back(
            mine(grad_all.reshape(2, all_tokens // 2, channels)),
            summed,
            own_unit_half[:, :channels],
            own_unit_half[:, channels : channels + 1] + own_unit_half[:, channels + 1 :],
            own_sums[0][:, None],
            own_sums[1][:, None],
        )
        grad_all = both_cores(new_half, 0).reshape(all_tokens, channels)
        grads[down - 2] = grad_all
    down, up = downs[-1], ups[-1]
    activated_own = jnp.concatenate([activated(s) for s in downs], axis=1)
    activated_all = all_ranks_aside(activated_own)
    act_grad = all_ranks(hidden_chain(down, up, grad_all))
    sides[up] = (units[up][:, :channels], act_grad)
    if ranks <= aside_limit:
        activated_all = jnp.concatenate(activated_all, axis=0)
        activated_all = lax.optimization_barrier(activated_all)
    for i, s in enumerate(downs):
        sides[s] = (turned(grads[s]), activated_all[:, i * width : (i + 1) * width])
    weight_grads = [
        lax.optimization_barrier(dot32(*pair, ((0,), (0,))).astype(jnp.bfloat16)) for pair in sides
    ]

    back, own_rows = sum_to_rows(input_grad(up, act_grad), grad_all)
    unit, inv_std = centred_unit(last_in)
    last_rows = norm_back(
        own_rows,
        back,
        unit,
        inv_std,
        jnp.mean(back, axis=-1, keepdims=True),
        jnp.mean(back * unit, axis=-1, keepdims=True),
    )

    def placed(out, block, source):
        block = (block.astype(jnp.float32) * gain_rows).astype(jnp.bfloat16)
        return lax.dynamic_update_slice_in_dim(out, block, lookup(starts, source), 1)

    weight_out = jnp.zeros((channels, hidden), jnp.bfloat16)
    weight_out = placed(weight_out, choose(column, weight_grads), column)
    last_grad = weight_grads[0]
    arrived = {}
    for d in range(1, columns):
        early = after(choose(partner(column, d, columns), [weight_grads[1]] + weight_grads[1:]))
        arrived[d] = swap_columns(early, d, lambda a, b: b > 0)
    if columns == 4:
        cut = channels // 32 * 16
        relayed = swap_columns(last_grad[cut:], 2, lambda a, b: a == 3)
    late = {}
    for d in (2, 3, 1) if columns == 4 else range(1, columns):
        if columns == 4 and d == 3:
            direct = swap_columns(last_grad[:cut], 3, lambda a, b: b == 0)
            relayed = swap_columns(relayed, 1, lambda a, b: b == 0)
            late[d] = jnp.concatenate([direct, relayed], axis=0)
        else:
            late[d] = swap_columns(last_grad, d, lambda a, b: b == 0)
    for d in range(1, columns):
        block = jnp.where(column == 0, late[d], arrived[d])
        weight_out = placed(weight_out, block, partner(column, d, columns))

    rows_of = [last_rows] + [own_rows] * (sections - 1)
    rows_got = [choose(column, rows_of)]
    for d in range(1, columns):
        sent = choose(partner(column, d, columns), rows_of)
        rows_got.append(swap_columns(sent, d, lambda a, b: b < sections - 1))
    rows_got = jnp.stack([choose(partner(column, m, columns), rows_got) for m in range(columns)])
    rows_got = both_cores(rows_got, 1).reshape(tokens, model_width)
    section_out = jnp.where(column == sections - 1, top_rows, rows_got)
    return (weight_out[None], section_out.reshape(1, micro_count, row_count, model_width))


def solution(mesh):
    in_specs = (
        P(None, "dp", None),
        P(None, "dp", None),
        P("dp", None),
        P("pipe", None, "dp", None),
        P("pipe", None, "dp", "tensor"),
        P("pipe", "dp", "tensor"),
        P("pipe", None),
    )
    out_specs = (P("pipe", "dp", "tensor"), P("pipe", None, "dp", None))
    return jax.shard_map(layer, mesh=mesh, in_specs=in_specs, out_specs=out_specs, check_vma=False)
```

time: 366 us -> 300 us (0.82)
  blocking collectives: 102 us -> 0 us
  starting transfers between devices: 42.5 us -> 90.7 us
  waiting for transfers between devices: 171 us -> 136 us
  local copies, waits for them, and re-layouts: 15.1 us -> 25.6 us
  other arithmetic: 19.3 us -> 27.2 us
  matrix products: 12.8 us -> 17.2 us
    all_to_all x11 -> x8, waiting for transfers between devices: 167 us -> 63.9 us  [exchange(): return lax.all_to_all(blocks, axes, 0, 0, tiled=True)]
    all_to_all x4 -> x0, blocking collectives: 102 us -> none  [exchange(): return lax.all_to_all(blocks, axes, 0, 0, tiled=True)]
    ppermute x0 -> x29, waiting for transfers between devices: none -> 69.8 us  [the longest x26 48.9 us: swap_columns(): return lax.ppermute(block, 'pipe', route)]
    ppermute x0 -> x29, starting transfers between devices: none -> 55.7 us  [the longest x26 50.8 us: swap_columns(): return lax.ppermute(block, 'pipe', route)]
    all_to_all x11 -> x8, starting transfers between devices: 42.3 us -> 34.6 us  [exchange(): return lax.all_to_all(blocks, axes, 0, 0, tiled=True)]
    dynamic_update_slice x0 -> x4, other arithmetic: none -> 6.85 us  [placed(): lax.dynamic_update_slice_in_dim(out, block, lookup(starts, source), 1)]
    dot_general x8, matrix products: 11.5 us -> 15.8 us  [dot32(): lax.dot_general(left, right, (dims, ((), ())), preferred_element_type=jnp...]
    select_n x1 -> x8, other arithmetic: 0.73 us -> 4.51 us  [the longest x4 3.58 us: choose(): return lax.select_n(which, *blocks)]
  transfers between devices with their start and end apart: 16 -> 43, of which waited for: 14 -> 23; matrix products, arithmetic and copies ran while one was open for 6% -> 18% of each run, Pallas kernels for 0% -> 0%
where the time goes in v2:
time: 300 us; the launch traced here: 298 us
  waiting for transfers between devices  136 us (45%)
  starting transfers between devices  90.7 us (30%)
  other arithmetic  27.2 us (9%)
  local copies, waits for them, and re-layouts  25.6 us (9%)
  matrix products  17.2 us (6%)
    all_to_all x8, waiting for transfers between devices, exchange(): return lax.all_to_all(blocks, axes, 0, 0, tiled=True)  63.9 us
    ppermute x26, starting transfers between devices, swap_columns(): return lax.ppermute(block, 'pipe', route)  50.8 us
    ppermute x26, waiting for transfers between devices, swap_columns(): return lax.ppermute(block, 'pipe', route)  48.9 us
    all_to_all x8, starting transfers between devices, exchange(): return lax.all_to_all(blocks, axes, 0, 0, tiled=True)  34.6 us
    ppermute x3, waiting for transfers between devices, all_ranks_aside(): got.append(lax.ppermute(block, 'dp', route))  20.9 us
    dot_general x8, matrix products, dot32(): lax.dot_general(left, right, (dims, ((), ())), preferred_element_type=jnp...  15.8 us
    dynamic_update_slice x4, other arithmetic, placed(): lax.dynamic_update_slice_in_dim(out, block, lookup(starts, source), 1)  6.85 us
  transfers between devices with their start and end apart: 43, of which 23 were waited for; matrix products, arithmetic and copies ran while one was open for 18% of the time, Pallas kernels for 0%

profile of v2, /device:TPU:0, one launch (start us, length us, event | category | flops | bytes accessed | tf_op | source)
XLA Modules:
  0.0 298.2 jit_solution(9876531512285150276)
XLA Ops:
  4.7 6.3 %all-to-all-start.1 = ((bf16[4,128,416]{1,2,0:T(8,128)(2,1)}), bf16[4,128,416]{1,2,0:T(8,128)(2,1)S(1)}, u32[]{:S(2)}, u32[]{:S(2)}) async-start(bf16[4,128,416]{1,2,0:T(8,128)(2,1)} %copy.106), calls=%async_computation.1 | async-start | bytes 851968 | tf_op jit(solution)/shard_map/all_to_all | solution.py:47
  15.1 8.3 %all-to-all-done.1 = bf16[4,128,416]{1,2,0:T(8,128)(2,1)S(1)} async-done(((bf16[4,128,416]{1,2,0:T(8,128)(2,1)}), bf16[4,128,416]{1,2,0:T(8,128)(2,1)S(1)}, u32[]{:S(2)}, u32[]{:S(2)}) %all-to-all-start.1) | async-done | bytes 426016 | tf_op jit(solution)/shard_map/all_to_all | solution.py:47
  23.4 3.5 %all-to-all-start = ((bf16[4,128,418]{1,2,0:T(8,128)(2,1)}), bf16[4,128,418]{1,2,0:T(8,128)(2,1)S(1)}, u32[]{:S(2)}, u32[]{:S(2)}) async-start(bf16[4,128,418]{1,2,0:T(8,128)(2,1)} %copy.103), calls=%async_computation | async-start | bytes 868352 | tf_op jit(solution)/shard_map/all_to_all | solution.py:47
  26.9 3.6 %fusion.2 = (bf16[416,896]{1,0:T(8,128)(2,1)}, bf16[416,896]{1,0:T(8,128)(2,1)S(1)}, bf16[416,896]{1,0:T(8,128)(2,1)}, bf16[416,896]{1,0:T(8,128)(2,1)}) fusion(bf16[1,416,3200]{2,1,0:T(8,128)(2,1)} %param.12, s32[]{:T(128)S(6)} %select_n.729, f32[416]{0:T(512)S(1)} %bitcast.215, s32[]{:T(128)S(6)} %select_n.725, s32[]{:T(128)S(6)} %select_n.735, ...), kind=kLoop, calls=%fused_computation.9 | loop fusion | flops 4472832 | bytes 5965456 | tf_op jit(solution)/shard_map/convert_element_type | solution.py:184
  34.0 4.9 %all-to-all-done = bf16[4,128,418]{1,2,0:T(8,128)(2,1)S(1)} async-done(((bf16[4,128,418]{1,2,0:T(8,128)(2,1)}), bf16[4,128,418]{1,2,0:T(8,128)(2,1)S(1)}, u32[]{:S(2)}, u32[]{:S(2)}) %all-to-all-start) | async-done | bytes 428064 | tf_op jit(solution)/shard_map/all_to_all | solution.py:47
  40.1 10.3 %collective-permute-done = bf16[416,896]{1,0:T(8,128)(2,1)} collective-permute-done((bf16[416,896]{1,0:T(8,128)(2,1)}, bf16[416,896]{1,0:T(8,128)(2,1)}, u32[]{:S(2)}, u32[]{:S(2)}) %collective-permute-start) | collective-permute-done | bytes 745504 | tf_op jit(solution)/shard_map/ppermute | solution.py:72
  50.4 15.3 %collective-permute-done.1 = bf16[416,896]{1,0:T(8,128)(2,1)} collective-permute-done((bf16[416,896]{1,0:T(8,128)(2,1)}, bf16[416,896]{1,0:T(8,128)(2,1)}, u32[]{:S(2)}, u32[]{:S(2)}) %collective-permute-start.1) | collective-permute-done | bytes 745504 | tf_op jit(solution)/shard_map/ppermute | solution.py:72
  65.7 3.0 %convolution_convert_fusion.2 = bf16[512,896]{1,0:T(8,128)(2,1)} fusion(bf16[512,416]{0,1:T(8,128)(2,1)S(1)} %copy_bitcast_fusion.2, bf16[416,896]{1,0:T(8,128)(2,1)} %collective-permute-done.1, bf16[416,896]{1,0:T(8,128)(2,1)} %collective-permute-done.2, bf16[416,896]{1,0:T(8,128)(2,1)S(1)} %get-tuple-element.27, ...), kind=kOutput, calls=%fused_computation.17 | convolution fusion | flops 383258624 | bytes 4325379 | tf_op jit(solution)/shard_map/dot_general | solution.py:55
  68.7 4.9 %all-to-all-start.2 = ((bf16[4,128,896]{2,1,0:T(8,128)(2,1)}), bf16[4,128,896]{2,1,0:T(8,128)(2,1)S(1)}, u32[]{:S(2)}, u32[]{:S(2)}) async-start(bf16[4,128,896]{2,1,0:T(8,128)(2,1)} %bitcast.198), calls=%async_computation.2 | async-start | bytes 1835008 | tf_op jit(solution)/shard_map/all_to_all | solution.py:47
  74.4 3.7 %collective-permute-start.28 = (bf16[16,1664]{1,0:T(8,128)(2,1)}, bf16[16,1664]{1,0:T(8,128)(2,1)}, u32[]{:S(2)}, u32[]{:S(2)}) collective-permute-start(bf16[16,1664]{1,0:T(8,128)(2,1)} %get-tuple-element.70), channel_id=1, source_target_pairs={{0,8},{1,9},{2,10},{3,11},{4,12},{5,13},{6,14},{7,15}} | collective-permute-start | bytes 159752 | tf_op jit(solution)/shard_map/ppermute | solution.py:72
  82.2 3.4 %collective-permute-start.5 = (bf16[128,896]{1,0:T(8,128)(2,1)S(1)}, bf16[128,896]{1,0:T(8,128)(2,1)S(1)}, u32[]{:S(2)}, u32[]{:S(2)}) collective-permute-start(bf16[128,896]{1,0:T(8,128)(2,1)S(1)} %get-tuple-element.42), channel_id=1, source_target_pairs={{0,24},{8,16},{16,8},{24,0},{1,25},{9,17},{17,9},{25,1},{2,26},{10... | collective-permute-start | bytes 688136 | tf_op jit(solution)/shard_map/ppermute | solution.py:72
  89.5 2.5 collective-permute-done.4
  95.7 3.8 %all-to-all-start.3 = ((bf16[4,128,896]{2,1,0:T(8,128)(2,1)}), bf16[4,128,896]{2,1,0:T(8,128)(2,1)S(1)}, u32[]{:S(2)}, u32[]{:S(2)}) async-start(bf16[4,128,896]{2,1,0:T(8,128)(2,1)} %broadcast_in_dim.75), calls=%async_computation.3 | async-start | bytes 1835008 | tf_op jit(solution)/shard_map/all_to_all | solution.py:47
  99.7 3.6 %collective-permute-start.6 = (bf16[256,418]{0,1:T(8,128)(2,1)S(1)}, bf16[256,418]{0,1:T(8,128)(2,1)S(1)}, u32[]{:S(2)}, u32[]{:S(2)}) collective-permute-start(bf16[256,418]{0,1:T(8,128)(2,1)S(1)} %bitcast.202), channel_id=1, source_target_pairs={{0,8},{16,24},{1,9},{17,25},{2,10},{18,26},{3,11},{19,27},{4,12},{... | collective-permute-start | bytes 642056 | tf_op jit(solution)/shard_map/ppermute | solution.py:72
  103.3 2.8 collective-permute-start.7
  116.3 5.3 %all-to-all-done.3 = bf16[4,128,896]{2,1,0:T(8,128)(2,1)S(1)} async-done(((bf16[4,128,896]{2,1,0:T(8,128)(2,1)}), bf16[4,128,896]{2,1,0:T(8,128)(2,1)S(1)}, u32[]{:S(2)}, u32[]{:S(2)}) %all-to-all-start.3) | async-done | bytes 917536 | tf_op jit(solution)/shard_map/all_to_all | solution.py:47
  124.8 2.9 all-to-all-start.4
  132.9 3.0 all-to-all-done.4
  138.0 3.8 %collective-permute-done.13 = bf16[256,416]{0,1:T(8,128)(2,1)S(1)} collective-permute-done((bf16[256,416]{0,1:T(8,128)(2,1)S(1)}, bf16[256,416]{0,1:T(8,128)(2,1)S(1)}, u32[]{:S(2)}, u32[]{:S(2)}) %collective-permute-start.13) | collective-permute-done | bytes 213024 | tf_op jit(solution)/shard_map/ppermute | solution.py:72
  149.3 3.1 %convolution_convert_fusion.1 = bf16[512,896]{1,0:T(8,128)(2,1)} fusion(bf16[512,416]{0,1:T(8,128)(2,1)S(1)} %bitcast.213, bf16[416,896]{1,0:T(8,128)(2,1)} %collective-permute-done.1, bf16[416,896]{1,0:T(8,128)(2,1)} %collective-permute-done.2, bf16[416,896]{1,0:T(8,128)(2,1)S(1)} %copy-done.19, bf16[416,896]{1,0:T(8,128)(2,1)} %collective-permute-done, ...), kind=kOutput, calls=%fused_computation.16 | convolution fusion | flops 383258624 | bytes 4325379 | tf_op jit(solution)/shard_map/dot_general | solution.py:55
  152.4 3.6 %all-to-all-start.5 = ((bf16[4,128,896]{2,1,0:T(8,128)(2,1)}), bf16[4,128,896]{2,1,0:T(8,128)(2,1)S(1)}, u32[]{:S(2)}, u32[]{:S(2)}) async-start(bf16[4,128,896]{2,1,0:T(8,128)(2,1)} %bitcast.199), calls=%async_computation.5 | async-start | bytes 1835008 | tf_op jit(solution)/shard_map/all_to_all | solution.py:47
  159.9 19.7 %collective-permute-done.17 = bf16[128,1792]{1,0:T(8,128)(2,1)} collective-permute-done((bf16[128,1792]{1,0:T(8,128)(2,1)}, bf16[128,1792]{1,0:T(8,128)(2,1)}, u32[]{:S(2)}, u32[]{:S(2)}) %collective-permute-start.17) | collective-permute-done | bytes 458784 | tf_op jit(solution)/shard_map/ppermute | solution.py:167
  188.7 19.7 %all-to-all-done.5 = bf16[4,128,896]{2,1,0:T(8,128)(2,1)S(1)} async-done(((bf16[4,128,896]{2,1,0:T(8,128)(2,1)}), bf16[4,128,896]{2,1,0:T(8,128)(2,1)S(1)}, u32[]{:S(2)}, u32[]{:S(2)}) %all-to-all-start.5) | async-done | bytes 917536 | tf_op jit(solution)/shard_map/all_to_all | solution.py:47
  210.8 3.5 %all-to-all-start.6 = ((bf16[4,128,896]{2,1,0:T(8,128)(2,1)}), bf16[4,128,896]{2,1,0:T(8,128)(2,1)S(1)}, u32[]{:S(2)}, u32[]{:S(2)}) async-start(bf16[4,128,896]{2,1,0:T(8,128)(2,1)} %broadcast_in_dim.79), calls=%async_computation.6 | async-start | bytes 1835008 | tf_op jit(solution)/shard_map/all_to_all | solution.py:47
  218.8 3.9 %collective-permute-start.20 = (bf16[416,896]{1,0:T(8,128)(2,1)}, bf16[416,896]{1,0:T(8,128)(2,1)}, u32[]{:S(2)}, u32[]{:S(2)}) collective-permute-start(bf16[416,896]{1,0:T(8,128)(2,1)} %get-tuple-element.32), channel_id=1, source_target_pairs={{0,8},{16,24},{24,16},{1,9},{17,25},{25,17},{2,10},{18,26},{26,18}... | collective-permute-start | bytes 2236424 | tf_op jit(solution)/shard_map/ppermute | solution.py:72
  222.6 2.8 collective-permute-start.22
  225.4 2.6 collective-permute-start.26
  228.2 9.4 %all-to-all-done.6 = bf16[4,128,896]{2,1,0:T(8,128)(2,1)S(1)} async-done(((bf16[4,128,896]{2,1,0:T(8,128)(2,1)}), bf16[4,128,896]{2,1,0:T(8,128)(2,1)S(1)}, u32[]{:S(2)}, u32[]{:S(2)}) %all-to-all-start.6) | async-done | bytes 917536 | tf_op jit(solution)/shard_map/all_to_all | solution.py:47
  245.7 6.0 %all-to-all-start.7 = ((bf16[16,16,520]{2,1,0:T(8,128)(2,1)}), bf16[16,16,520]{2,1,0:T(8,128)(2,1)S(1)}, u32[]{:S(2)}, u32[]{:S(2)}) async-start(bf16[16,16,520]{2,1,0:T(8,128)(2,1)} %pad_maximum_fusion.6), calls=%async_computation.7 | async-start | bytes 655360 | tf_op jit(solution)/shard_map/all_to_all | solution.py:47
  255.5 12.3 %all-to-all-done.7 = bf16[16,16,520]{2,1,0:T(8,128)(2,1)S(1)} async-done(((bf16[16,16,520]{2,1,0:T(8,128)(2,1)}), bf16[16,16,520]{2,1,0:T(8,128)(2,1)S(1)}, u32[]{:S(2)}, u32[]{:S(2)}) %all-to-all-start.7) | async-done | bytes 266272 | tf_op jit(solution)/shard_map/all_to_all | solution.py:47
  275.1 6.0 %collective-permute-start.31 = (bf16[16,1664]{1,0:T(8,128)(2,1)S(1)}, bf16[16,1664]{1,0:T(8,128)(2,1)S(1)}, u32[]{:S(2)}, u32[]{:S(2)}) collective-permute-start(bf16[16,1664]{1,0:T(8,128)(2,1)S(1)} %get-tuple-element.14), channel_id=1, source_target_pairs={{0,8},{8,0},{24,16},{1,9},{9,1},{25,17},{2,10},{10,2},{26,18},{3,1... | collective-permute-start | bytes 159752 | tf_op jit(solution)/shard_map/ppermute | solution.py:72
  286.2 9.4 %collective-permute-done.23 = bf16[208,896]{1,0:T(8,128)(2,1)S(1)} collective-permute-done((bf16[208,896]{1,0:T(8,128)(2,1)S(1)}, bf16[208,896]{1,0:T(8,128)(2,1)S(1)}, u32[]{:S(2)}, u32[]{:S(2)}) %collective-permute-start.23) | collective-permute-done | bytes 372768 | tf_op jit(solution)/shard_map/ppermute | solution.py:72
  (223 shorter events, 99.4 us)
Async XLA Ops:
  4.7 18.7 %all-to-all-start.1 = ((bf16[4,128,416]{1,2,0:T(8,128)(2,1)}), bf16[4,128,416]{1,2,0:T(8,128)(2,1)S(1)}, u32[]{:S(2)}, u32[]{:S(2)}) async-start(bf16[4,128,416]{1,2,0:T(8,128)(2,1)} %copy.106), calls=%async_computation.1 | async-start | bytes 851968 | tf_op jit(solution)/shard_map/all_to_all | solution.py:47
  23.4 15.6 %all-to-all-start = ((bf16[4,128,418]{1,2,0:T(8,128)(2,1)}), bf16[4,128,418]{1,2,0:T(8,128)(2,1)S(1)}, u32[]{:S(2)}, u32[]{:S(2)}) async-start(bf16[4,128,418]{1,2,0:T(8,128)(2,1)} %copy.103), calls=%async_computation | async-start | bytes 868352 | tf_op jit(solution)/shard_map/all_to_all | solution.py:47
  30.5 19.9 %collective-permute-start = (bf16[416,896]{1,0:T(8,128)(2,1)}, bf16[416,896]{1,0:T(8,128)(2,1)}, u32[]{:S(2)}, u32[]{:S(2)}) collective-permute-start(bf16[416,896]{1,0:T(8,128)(2,1)} %get-tuple-element.26), channel_id=1, source_target_pairs={{0,8},{8,0},{16,24},{24,16},{1,9},{9,1},{17,25},{25,17},{2,10},{10... | collective-permute-start | bytes 2236424 | tf_op jit(solution)/shard_map/ppermute | solution.py:72
  32.0 33.7 %collective-permute-start.1 = (bf16[416,896]{1,0:T(8,128)(2,1)}, bf16[416,896]{1,0:T(8,128)(2,1)}, u32[]{:S(2)}, u32[]{:S(2)}) collective-permute-start(bf16[416,896]{1,0:T(8,128)(2,1)} %get-tuple-element.29), channel_id=1, source_target_pairs={{0,16},{8,24},{16,0},{24,8},{1,17},{9,25},{17,1},{25,9},{2,18},{10... | collective-permute-start | bytes 2236424 | tf_op jit(solution)/shard_map/ppermute | solution.py:72
  33.5 32.2 %collective-permute-start.2 = (bf16[416,896]{1,0:T(8,128)(2,1)}, bf16[416,896]{1,0:T(8,128)(2,1)}, u32[]{:S(2)}, u32[]{:S(2)}) collective-permute-start(bf16[416,896]{1,0:T(8,128)(2,1)} %get-tuple-element.28), channel_id=1, source_target_pairs={{0,24},{8,16},{16,8},{24,0},{1,25},{9,17},{17,9},{25,1},{2,26},{10... | collective-permute-start | bytes 2236424 | tf_op jit(solution)/shard_map/ppermute | solution.py:72
  68.7 25.7 %all-to-all-start.2 = ((bf16[4,128,896]{2,1,0:T(8,128)(2,1)}), bf16[4,128,896]{2,1,0:T(8,128)(2,1)S(1)}, u32[]{:S(2)}, u32[]{:S(2)}) async-start(bf16[4,128,896]{2,1,0:T(8,128)(2,1)} %bitcast.198), calls=%async_computation.2 | async-start | bytes 1835008 | tf_op jit(solution)/shard_map/all_to_all | solution.py:47
  82.1 9.9 %collective-permute-start.4 = (bf16[128,896]{1,0:T(8,128)(2,1)S(1)}, bf16[128,896]{1,0:T(8,128)(2,1)S(1)}, u32[]{:S(2)}, u32[]{:S(2)}) collective-permute-start(bf16[128,896]{1,0:T(8,128)(2,1)S(1)} %get-tuple-element.43), channel_id=1, source_target_pairs={{0,16},{8,24},{16,0},{24,8},{1,17},{9,25},{17,1},{25,9},{2,18},{10... | collective-permute-start | bytes 688136 | tf_op jit(solution)/shard_map/ppermute | solution.py:72
  82.2 9.8 %collective-permute-start.5 = (bf16[128,896]{1,0:T(8,128)(2,1)S(1)}, bf16[128,896]{1,0:T(8,128)(2,1)S(1)}, u32[]{:S(2)}, u32[]{:S(2)}) collective-permute-start(bf16[128,896]{1,0:T(8,128)(2,1)S(1)} %get-tuple-element.42), channel_id=1, source_target_pairs={{0,24},{8,16},{16,8},{24,0},{1,25},{9,17},{17,9},{25,1},{2,26},{10... | collective-permute-start | bytes 688136 | tf_op jit(solution)/shard_map/ppermute | solution.py:72
  95.7 25.9 %all-to-all-start.3 = ((bf16[4,128,896]{2,1,0:T(8,128)(2,1)}), bf16[4,128,896]{2,1,0:T(8,128)(2,1)S(1)}, u32[]{:S(2)}, u32[]{:S(2)}) async-start(bf16[4,128,896]{2,1,0:T(8,128)(2,1)} %broadcast_in_dim.75), calls=%async_computation.3 | async-start | bytes 1835008 | tf_op jit(solution)/shard_map/all_to_all | solution.py:47
  99.7 10.2 %collective-permute-start.6 = (bf16[256,418]{0,1:T(8,128)(2,1)S(1)}, bf16[256,418]{0,1:T(8,128)(2,1)S(1)}, u32[]{:S(2)}, u32[]{:S(2)}) collective-permute-start(bf16[256,418]{0,1:T(8,128)(2,1)S(1)} %bitcast.202), channel_id=1, source_target_pairs={{0,8},{16,24},{1,9},{17,25},{2,10},{18,26},{3,11},{19,27},{4,12},{... | collective-permute-start | bytes 642056 | tf_op jit(solution)/shard_map/ppermute | solution.py:72
  124.8 11.1 %all-to-all-start.4 = ((f32[32,8,128]{2,1,0:T(8,128)}), f32[32,8,128]{2,1,0:T(8,128)S(1)}, u32[]{:S(2)}, u32[]{:S(2)}) async-start(f32[32,8,128]{2,1,0:T(8,128)} %broadcast_in_dim.78), calls=%async_computation.4 | async-start | bytes 262144 | tf_op jit(solution)/shard_map/all_to_all | solution.py:47
  129.4 8.7 %collective-permute-start.12 = (bf16[256,416]{0,1:T(8,128)(2,1)S(1)}, bf16[256,416]{0,1:T(8,128)(2,1)S(1)}, u32[]{:S(2)}, u32[]{:S(2)}) collective-permute-start(bf16[256,416]{0,1:T(8,128)(2,1)S(1)} %add_convert_fusion), channel_id=1, source_target_pairs={{0,8},{8,0},{16,24},{24,16},{1,9},{9,1},{17,25},{25,17},{2,10},{10... | collective-permute-start | bytes 638984 | tf_op jit(solution)/shard_map/ppermute | solution.py:72
  131.0 10.8 %collective-permute-start.13 = (bf16[256,416]{0,1:T(8,128)(2,1)S(1)}, bf16[256,416]{0,1:T(8,128)(2,1)S(1)}, u32[]{:S(2)}, u32[]{:S(2)}) collective-permute-start(bf16[256,416]{0,1:T(8,128)(2,1)S(1)} %add_convert_fusion), channel_id=1, source_target_pairs={{0,16},{8,24},{16,0},{24,8},{1,17},{9,25},{17,1},{25,9},{2,18},{10... | collective-permute-start | bytes 638984 | tf_op jit(solution)/shard_map/ppermute | solution.py:72
  132.5 10.6 %collective-permute-start.14 = (bf16[256,416]{0,1:T(8,128)(2,1)S(1)}, bf16[256,416]{0,1:T(8,128)(2,1)S(1)}, u32[]{:S(2)}, u32[]{:S(2)}) collective-permute-start(bf16[256,416]{0,1:T(8,128)(2,1)S(1)} %add_convert_fusion), channel_id=1, source_target_pairs={{0,24},{8,16},{16,8},{24,0},{1,25},{9,17},{17,9},{25,1},{2,26},{10... | collective-permute-start | bytes 638984 | tf_op jit(solution)/shard_map/ppermute | solution.py:72
  144.2 15.6 %collective-permute-start.16 = (bf16[128,1792]{1,0:T(8,128)(2,1)}, bf16[128,1792]{1,0:T(8,128)(2,1)}, u32[]{:S(2)}, u32[]{:S(2)}) collective-permute-start(bf16[128,1792]{1,0:T(8,128)(2,1)} %pad_maximum_fusion.1), channel_id=1, source_target_pairs={{0,2},{2,4},{4,6},{6,0},{1,3},{3,5},{5,7},{7,1},{8,10},{10,12},{12... | collective-permute-start | bytes 1376264 | tf_op jit(solution)/shard_map/ppermute | solution.py:167
  145.5 34.1 %collective-permute-start.17 = (bf16[128,1792]{1,0:T(8,128)(2,1)}, bf16[128,1792]{1,0:T(8,128)(2,1)}, u32[]{:S(2)}, u32[]{:S(2)}) collective-permute-start(bf16[128,1792]{1,0:T(8,128)(2,1)} %pad_maximum_fusion.1), channel_id=1, source_target_pairs={{0,4},{2,6},{4,0},{6,2},{1,5},{3,7},{5,1},{7,3},{8,12},{10,14},{12... | collective-permute-start | bytes 1376264 | tf_op jit(solution)/shard_map/ppermute | solution.py:167
  147.7 31.9 %collective-permute-start.18 = (bf16[128,1792]{1,0:T(8,128)(2,1)}, bf16[128,1792]{1,0:T(8,128)(2,1)}, u32[]{:S(2)}, u32[]{:S(2)}) collective-permute-start(bf16[128,1792]{1,0:T(8,128)(2,1)} %pad_maximum_fusion.1), channel_id=1, source_target_pairs={{0,6},{2,0},{4,2},{6,4},{1,7},{3,1},{5,3},{7,5},{8,14},{10,8},{12,... | collective-permute-start | bytes 1376264 | tf_op jit(solution)/shard_map/ppermute | solution.py:167
  152.4 56.0 %all-to-all-start.5 = ((bf16[4,128,896]{2,1,0:T(8,128)(2,1)}), bf16[4,128,896]{2,1,0:T(8,128)(2,1)S(1)}, u32[]{:S(2)}, u32[]{:S(2)}) async-start(bf16[4,128,896]{2,1,0:T(8,128)(2,1)} %bitcast.199), calls=%async_computation.5 | async-start | bytes 1835008 | tf_op jit(solution)/shard_map/all_to_all | solution.py:47
  210.8 26.9 %all-to-all-start.6 = ((bf16[4,128,896]{2,1,0:T(8,128)(2,1)}), bf16[4,128,896]{2,1,0:T(8,128)(2,1)S(1)}, u32[]{:S(2)}, u32[]{:S(2)}) async-start(bf16[4,128,896]{2,1,0:T(8,128)(2,1)} %broadcast_in_dim.79), calls=%async_computation.6 | async-start | bytes 1835008 | tf_op jit(solution)/shard_map/all_to_all | solution.py:47
  218.8 50.2 %collective-permute-start.20 = (bf16[416,896]{1,0:T(8,128)(2,1)}, bf16[416,896]{1,0:T(8,128)(2,1)}, u32[]{:S(2)}, u32[]{:S(2)}) collective-permute-start(bf16[416,896]{1,0:T(8,128)(2,1)} %get-tuple-element.32), channel_id=1, source_target_pairs={{0,8},{16,24},{24,16},{1,9},{17,25},{25,17},{2,10},{18,26},{26,18}... | collective-permute-start | bytes 2236424 | tf_op jit(solution)/shard_map/ppermute | solution.py:72
  222.6 51.2 %collective-permute-start.22 = (bf16[416,896]{1,0:T(8,128)(2,1)}, bf16[416,896]{1,0:T(8,128)(2,1)}, u32[]{:S(2)}, u32[]{:S(2)}) collective-permute-start(bf16[416,896]{1,0:T(8,128)(2,1)} %get-tuple-element.31), channel_id=1, source_target_pairs={{0,16},{8,24},{24,8},{1,17},{9,25},{25,9},{2,18},{10,26},{26,10},{... | collective-permute-start | bytes 2236424 | tf_op jit(solution)/shard_map/ppermute | solution.py:72
  225.4 60.8 %collective-permute-start.26 = (bf16[416,896]{1,0:T(8,128)(2,1)}, bf16[416,896]{1,0:T(8,128)(2,1)}, u32[]{:S(2)}, u32[]{:S(2)}) collective-permute-start(bf16[416,896]{1,0:T(8,128)(2,1)} %get-tuple-element.30), channel_id=1, source_target_pairs={{0,24},{8,16},{16,8},{1,25},{9,17},{17,9},{2,26},{10,18},{18,10},{... | collective-permute-start | bytes 2236424 | tf_op jit(solution)/shard_map/ppermute | solution.py:72
  242.1 27.6 %collective-permute-start.19 = (bf16[416,896]{1,0:T(8,128)(2,1)S(1)}, bf16[416,896]{1,0:T(8,128)(2,1)}, u32[]{:S(2)}, u32[]{:S(2)}) collective-permute-start(bf16[416,896]{1,0:T(8,128)(2,1)S(1)} %convolution_convert_fusion.6), channel_id=1, source_target_pairs={{8,0},{9,1},{10,2},{11,3},{12,4},{13,5},{14,6},{15,7}} | collective-permute-start | bytes 2236424 | tf_op jit(solution)/shard_map/ppermute | solution.py:72
  243.4 31.7 %collective-permute-start.21 = (bf16[416,896]{1,0:T(8,128)(2,1)S(1)}, bf16[416,896]{1,0:T(8,128)(2,1)}, u32[]{:S(2)}, u32[]{:S(2)}) collective-permute-start(bf16[416,896]{1,0:T(8,128)(2,1)S(1)} %convolution_convert_fusion.6), channel_id=1, source_target_pairs={{16,0},{17,1},{18,2},{19,3},{20,4},{21,5},{22,6},{23,7}} | collective-permute-start | bytes 2236424 | tf_op jit(solution)/shard_map/ppermute | solution.py:72
  245.7 22.2 %all-to-all-start.7 = ((bf16[16,16,520]{2,1,0:T(8,128)(2,1)}), bf16[16,16,520]{2,1,0:T(8,128)(2,1)S(1)}, u32[]{:S(2)}, u32[]{:S(2)}) async-start(bf16[16,16,520]{2,1,0:T(8,128)(2,1)} %pad_maximum_fusion.6), calls=%async_computation.7 | async-start | bytes 655360 | tf_op jit(solution)/shard_map/all_to_all | solution.py:47
  269.0 14.4 %collective-permute-start.24 = (bf16[208,896]{1,0:T(8,128)(2,1)S(1)}, bf16[208,896]{1,0:T(8,128)(2,1)S(1)}, u32[]{:S(2)}, u32[]{:S(2)}) collective-permute-start(bf16[208,896]{1,0:T(8,128)(2,1)S(1)} %copy-done.22), channel_id=1, source_target_pairs={{24,8},{25,9},{26,10},{27,11},{28,12},{29,13},{30,14},{31,15}} | collective-permute-start | bytes 1118216 | tf_op jit(solution)/shard_map/ppermute | solution.py:72
  269.7 15.0 %collective-permute-start.32 = (bf16[16,1664]{1,0:T(8,128)(2,1)S(1)}, bf16[16,1664]{1,0:T(8,128)(2,1)S(1)}, u32[]{:S(2)}, u32[]{:S(2)}) collective-permute-start(bf16[16,1664]{1,0:T(8,128)(2,1)S(1)} %get-tuple-element.74), channel_id=1, source_target_pairs={{0,16},{16,0},{24,8},{1,17},{17,1},{25,9},{2,18},{18,2},{26,10},{3... | collective-permute-start | bytes 159752 | tf_op jit(solution)/shard_map/ppermute | solution.py:72
  273.8 12.1 %collective-permute-start.33 = (bf16[16,1664]{1,0:T(8,128)(2,1)S(1)}, bf16[16,1664]{1,0:T(8,128)(2,1)S(1)}, u32[]{:S(2)}, u32[]{:S(2)}) collective-permute-start(bf16[16,1664]{1,0:T(8,128)(2,1)S(1)} %get-tuple-element.73), channel_id=1, source_target_pairs={{8,16},{16,8},{24,0},{9,17},{17,9},{25,1},{10,18},{18,10},{26,2},{... | collective-permute-start | bytes 159752 | tf_op jit(solution)/shard_map/ppermute | solution.py:72
  275.1 10.9 %collective-permute-start.31 = (bf16[16,1664]{1,0:T(8,128)(2,1)S(1)}, bf16[16,1664]{1,0:T(8,128)(2,1)S(1)}, u32[]{:S(2)}, u32[]{:S(2)}) collective-permute-start(bf16[16,1664]{1,0:T(8,128)(2,1)S(1)} %get-tuple-element.14), channel_id=1, source_target_pairs={{0,8},{8,0},{24,16},{1,9},{9,1},{25,17},{2,10},{10,2},{26,18},{3,1... | collective-permute-start | bytes 159752 | tf_op jit(solution)/shard_map/ppermute | solution.py:72
  283.4 12.3 %collective-permute-start.23 = (bf16[208,896]{1,0:T(8,128)(2,1)S(1)}, bf16[208,896]{1,0:T(8,128)(2,1)S(1)}, u32[]{:S(2)}, u32[]{:S(2)}) collective-permute-start(bf16[208,896]{1,0:T(8,128)(2,1)S(1)} %get-tuple-element.44), channel_id=1, source_target_pairs={{24,0},{25,1},{26,2},{27,3},{28,4},{29,5},{30,6},{31,7}} | collective-permute-start | bytes 1118216 | tf_op jit(solution)/shard_map/ppermute | solution.py:72
  284.7 11.4 %collective-permute-start.25 = (bf16[208,896]{1,0:T(8,128)(2,1)S(1)}, bf16[208,896]{1,0:T(8,128)(2,1)S(1)}, u32[]{:S(2)}, u32[]{:S(2)}) collective-permute-start(bf16[208,896]{1,0:T(8,128)(2,1)S(1)} %collective-permute-done.24), channel_id=1, source_target_pairs={{8,0},{9,1},{10,2},{11,3},{12,4},{13,5},{14,6},{15,7}} | collective-permute-start | bytes 1118216 | tf_op jit(solution)/shard_map/ppermute | solution.py:72
  286.1 11.0 %collective-permute-start.34 = (bf16[4,16,1664]{2,1,0:T(8,128)(2,1)S(1)}, bf16[4,16,1664]{2,1,0:T(8,128)(2,1)S(1)}, u32[]{:S(2)}, u32[]{:S(2)}) collective-permute-start(bf16[4,16,1664]{2,1,0:T(8,128)(2,1)S(1)} %pad_maximum_fusion.7), channel_id=1, source_target_pairs={{0,1},{1,0},{2,3},{3,2},{4,5},{5,4},{6,7},{7,6},{8,9},{9,8},{10,11... | collective-permute-start | bytes 638984 | tf_op jit(solution)/shard_map/ppermute | solution.py:51
  (37 other events, 291.9 us)

commit v3 on v2

--- a/solution.py
+++ b/solution.py
@@ -138,16 +138,37 @@
         halves = block.reshape(ranks * columns, 2, part, channels)
         return halves[:, 0], halves[:, 1]
 
-    def sum_to_rows(partial_sum, whole):
+    def to_channels_aside(rows, finish):
+        if ranks > aside_limit:
+            blocks = [finish(rows[:, j]) for j in range(ranks)]
+            return exchange(jnp.stack(blocks), "dp")
+        got = []
+        for distance in range(ranks):
+            to = (rank + distance) % ranks
+            block = finish(lax.dynamic_index_in_dim(rows, to, 1, keepdims=False))
+            if distance > 0:
+                route = [(i, (i + distance) % ranks) for i in range(ranks)]
+                block = lax.ppermute(block, "dp", route)
+            got.append(block)
+        by_rank = [choose((rank + ranks - j) % ranks, got) for j in range(ranks)]
+        return jnp.stack(by_rank)
+
+    def sum_to_rows(partial_sum, *wholes):
         halves = token_halves(partial_sum)
         given = theirs(halves).astype(jnp.bfloat16)
         pair = (mine(halves) + swap_cores(given).astype(jnp.float32)).astype(jnp.bfloat16)
-        share = lax.dynamic_slice_in_dim(mine(token_halves(whole)), column * piece, piece, 2)
-        got = exchange(jnp.concatenate([pair, share], axis=-1), ("dp", "pipe"))
-        got = got.reshape(ranks, columns, part, channels + piece)
+        shares = [
+            lax.dynamic_slice_in_dim(mine(token_halves(whole)), column * piece, piece, 2)
+            for whole in wholes
+        ]
+        got = exchange(jnp.concatenate([pair] + shares, axis=-1), ("dp", "pipe"))
+        got = got.reshape(ranks, columns, part, channels + len(wholes) * piece)
         summed = jnp.sum(got[..., :channels].astype(jnp.float32), axis=1)
-        summed = summed.transpose(1, 0, 2).reshape(part, model_width)
-        return summed, got[..., channels:].transpose(2, 0, 1, 3).reshape(part, model_width)
+        rows = [summed.transpose(1, 0, 2).reshape(part, model_width)]
+        for i in range(len(wholes)):
+            share = got[..., channels + i * piece : channels + (i + 1) * piece]
+            rows.append(share.transpose(2, 0, 1, 3).reshape(part, model_width))
+        return rows
 
     def sum_over_ranks(partial_sum):
         sent = partial_sum.astype(jnp.bfloat16).reshape(ranks, tokens, -1)
@@ -177,45 +198,75 @@
         ]
         return jnp.concatenate(order, axis=0)
 
+    def core_half(rows):
+        return mine(rows.reshape(2, tokens // 2, ranks, channels))
+
+    def both_halves(block):
+        return both_cores(block, 1).reshape(all_tokens, -1)
+
     def to_channels(rows):
-        return exchange(rows.transpose(1, 0, 2), "dp").reshape(all_tokens, -1)
-
-    weight_got = scatter_hidden(
-        weights[0], lambda block: (block.astype(jnp.float32) * gain_rows).astype(jnp.bfloat16)
-    )
+        return exchange(rows.transpose(1, 0, 2), "dp")
+
+    top = sections - 1
+    cut = channels // 32 * 16
+
+    def weight_piece(distance):
+        block = hidden_piece(weights[0], partner(column, distance, columns))
+        return (block.astype(jnp.float32) * gain_rows).astype(jnp.bfloat16)
+
+    weight_pieces = [weight_piece(d) for d in range(columns)]
+    top_weight = [weight_pieces[0]] * columns
+    if columns == 4:
+        from_top = lambda a, b: a == top
+        over_2 = swap_columns(weight_pieces[3][:cut], 1, from_top)
+        over_1 = swap_columns(weight_pieces[3][cut:], 2, from_top)
+        top_weight[2] = swap_columns(weight_pieces[1], 1, from_top)
+        top_weight[1] = swap_columns(weight_pieces[2], 2, from_top)
+        over_2 = swap_columns(over_2, 2, lambda a, b: b == 0)
+        over_1 = swap_columns(over_1, 1, lambda a, b: b == 0)
+        top_weight[0] = jnp.concatenate([over_2, over_1], axis=0)
+    else:
+        for d in range(1, columns):
+            top_weight[partner(top, d, columns)] = swap_columns(
+                weight_pieces[d], d, lambda a, b: a == top
+            )
+    top_weight = choose(column, top_weight)
     top_rows = local_top(llm_grad, slot_row[:, 0], counts[0]).reshape(tokens, model_width)
-    grad_all = to_channels(top_rows.reshape(tokens, ranks, channels))
+    grad_all = both_halves(to_channels(core_half(top_rows)))
 
     own_in = saved_in[0].reshape(tokens, model_width)
     own_unit, own_std = centred_unit(own_in)
-    std_terms = jnp.stack(exact_halves(own_std), axis=-1)
-    unit_sent = jnp.concatenate(
-        [
-            own_unit.astype(jnp.bfloat16).reshape(tokens, ranks, channels),
-            jnp.broadcast_to(std_terms, (tokens, ranks, 2)),
-        ],
-        axis=-1,
-    )
-    unit_half = mine(to_channels(unit_sent).reshape(2, all_tokens // 2, channels + 2))
-    grad_all = after(grad_all, unit_half)
-
-    pre_flat = after(saved_pre[0].reshape(tokens, hidden), *weight_got)
-    pre_parts = by_section(scatter_hidden(pre_flat))
-    weight_parts = by_section(weight_got)
-    unit_half = after(unit_half, *pre_parts)
+    std_terms = [mine(term.reshape(2, tokens // 2, 1)) for term in exact_halves(own_std)]
+    wide = -(-(channels + 2) // lanes) * lanes
+    lane = lax.broadcasted_iota(jnp.int32, (tokens // 2, wide), 1)
+
+    def with_std(block):
+        block = jnp.pad(block, [(0, 0), (0, wide - channels)])
+        block = jnp.where(lane == channels, std_terms[0], block)
+        return jnp.where(lane == channels + 1, std_terms[1], block)
+
+    unit_half = to_channels_aside(core_half(own_unit.astype(jnp.bfloat16)), with_std)
+
+    pre_parts = by_section(scatter_hidden(saved_pre[0].reshape(tokens, hidden)))
+    weight_got = [weight_pieces[0]] + [
+        swap_columns(weight_pieces[d], d, lambda a, b: a != top)
+        for d in range(1, columns)
+    ]
+    weight_parts = by_section(weight_got)[:top]
+    weight_parts = by_section(weight_got)[: top - 1] + weight_parts[top - 1 :]
+    weight_parts = [lax.optimization_barrier(part) for part in weight_parts[: top - 1]] + [
+        weight_parts[top - 1],
+        top_weight,
+    ]
     unit_got = [unit_half] + [
         swap_columns(unit_half, d, lambda a, b: a % 2 == 0) for d in range(1, columns)
     ]
-    units = {s: both_cores(choose(partner(column, s, columns), unit_got), 0) for s in ups}
-    units = {s: unit.reshape(all_tokens, channels + 2) for s, unit in units.items()}
-    in_halves = own_in.reshape(columns, 2, part, model_width)
-    in_halves = jnp.where(core == 0, in_halves[:, 0], in_halves[:, 1])
-    in_got = [lax.dynamic_index_in_dim(in_halves, column, 0, keepdims=False)]
-    for d in range(1, columns):
-        to = partner(column, d, columns)
-        sent = lax.dynamic_index_in_dim(in_halves, to, 0, keepdims=False)
-        in_got.append(swap_columns(sent, d, lambda a, b: a == 0))
-    last_in = choose(column, in_got)
+    units = {s: both_halves(choose(partner(column, s, columns), unit_got)) for s in ups}
+    stds = {
+        s: jnp.sum(block[:, channels : channels + 2].astype(jnp.float32), axis=1, keepdims=True)
+        for s, block in units.items()
+    }
+    units = {s: block[:, :channels] for s, block in units.items()}
 
     def hidden_chain(down, up, grad):
         partial_hidden = dot32(grad, weight_parts[down], ((1,), (0,)))
@@ -238,39 +289,38 @@
     grads = {downs[0]: grad_all}
     for up, down in zip(ups[:-1], downs):
         act_grad = all_ranks(hidden_chain(down, up, grad_all))
-        sides[up] = (units[up][:, :channels], act_grad)
+        sides[up] = (units[up], act_grad)
         back = input_grad(up, act_grad)
-        unit = units[up][:, :channels].astype(jnp.float32)
+        unit = units[up].astype(jnp.float32)
         sums = jnp.stack([jnp.sum(back, axis=1), jnp.sum(back * unit, axis=1)])
         sums = sums.reshape(2 * all_tokens // lanes, lanes)
         devices = ranks * columns * 2
         sums = exchange(
             jnp.broadcast_to(sums[None], (devices,) + sums.shape), ("dp", "pipe", "tensor")
         )
-        sums = (jnp.sum(sums, axis=0) / model_width).reshape(2, all_tokens)
+        sums = jnp.sum(sums, axis=0).reshape(2, all_tokens)
         halves = back.reshape(2, all_tokens // 2, channels)
         pair = mine(halves) + swap_cores(theirs(halves).astype(jnp.bfloat16)).astype(jnp.float32)
         pair = pair.astype(jnp.bfloat16)
         summed = pair.astype(jnp.float32)
         for d in range(1, columns):
             summed = summed + swap_columns(pair, d).astype(jnp.float32)
-        own_unit_half = mine(units[up].reshape(2, all_tokens // 2, channels + 2)).astype(jnp.float32)
-        own_sums = mine(sums.reshape(2, 2, all_tokens // 2).transpose(1, 0, 2))
+        own_sums = mine(sums.reshape(2, 2, all_tokens // 2).transpose(1, 0, 2))[:, :, None]
         new_half = norm_back(
             mine(grad_all.reshape(2, all_tokens // 2, channels)),
             summed,
-            own_unit_half[:, :channels],
-            own_unit_half[:, channels : channels + 1] + own_unit_half[:, channels + 1 :],
-            own_sums[0][:, None],
-            own_sums[1][:, None],
+            mine(units[up].reshape(2, all_tokens // 2, channels)).astype(jnp.float32),
+            mine(stds[up].reshape(2, all_tokens // 2, 1)),
+            own_sums[0] / model_width,
+            own_sums[1] / model_width,
         )
         grad_all = both_cores(new_half, 0).reshape(all_tokens, channels)
         grads[down - 2] = grad_all
     down, up = downs[-1], ups[-1]
     activated_own = jnp.concatenate([activated(s) for s in downs], axis=1)
-    activated_all = all_ranks_aside(activated_own)
+    activated_all = all_ranks_aside(lax.optimization_barrier(activated_own))
     act_grad = all_ranks(hidden_chain(down, up, grad_all))
-    sides[up] = (units[up][:, :channels], act_grad)
+    sides[up] = (units[up], act_grad)
     if ranks <= aside_limit:
         activated_all = jnp.concatenate(activated_all, axis=0)
         activated_all = lax.optimization_barrier(activated_all)
@@ -280,8 +330,11 @@
         lax.optimization_barrier(dot32(*pair, ((0,), (0,))).astype(jnp.bfloat16)) for pair in sides
     ]
 
-    back, own_rows = sum_to_rows(input_grad(up, act_grad), grad_all)
-    unit, inv_std = centred_unit(last_in)
+    back, own_rows, unit = sum_to_rows(input_grad(up, act_grad), grad_all, units[up])
+    unit = unit.astype(jnp.float32)
+    inv_std = lax.dynamic_slice_in_dim(
+        stds[up], rank * tokens + (2 * column + core) * part, part, 0
+    )
     last_rows = norm_back(
         own_rows,
         back,
@@ -303,7 +356,6 @@
         early = after(choose(partner(column, d, columns), [weight_grads[1]] + weight_grads[1:]))
         arrived[d] = swap_columns(early, d, lambda a, b: b > 0)
     if columns == 4:
-        cut = channels // 32 * 16
         relayed = swap_columns(last_grad[cut:], 2, lambda a, b: a == 3)
     late = {}
     for d in (2, 3, 1) if columns == 4 else range(1, columns):
@@ -318,11 +370,7 @@
         weight_out = placed(weight_out, block, partner(column, d, columns))
 
     rows_of = [last_rows] + [own_rows] * (sections - 1)
-    rows_got = [choose(column, rows_of)]
-    for d in range(1, columns):
-        sent = choose(partner(column, d, columns), rows_of)
-        rows_got.append(swap_columns(sent, d, lambda a, b: b < sections - 1))
-    rows_got = jnp.stack([choose(partner(column, m, columns), rows_got) for m in range(columns)])
+    rows_got = exchange(jnp.stack(rows_of), "pipe")
     rows_got = both_cores(rows_got, 1).reshape(tokens, model_width)
     section_out = jnp.where(column == sections - 1, top_rows, rows_got)
     return (weight_out[None], section_out.reshape(1, micro_count, row_count, model_width))

time: 300 us -> 322 us (1.073)
  starting transfers between devices: 90.7 us -> 110 us
  other arithmetic: 27.2 us -> 37.1 us
  waiting for transfers between devices: 136 us -> 132 us
    all_to_all x8, waiting for transfers between devices: 63.9 us -> 15.2 us  [exchange(): return lax.all_to_all(blocks, axes, 0, 0, tiled=True)]
    ppermute x3, waiting for transfers between devices: 20.9 us -> 42.6 us  [all_ranks_aside(): got.append(lax.ppermute(block, 'dp', route))]
    ppermute x0 -> x3, waiting for transfers between devices: none -> 19.2 us  [to_channels_aside(): block = lax.ppermute(block, 'dp', route)]
    all_to_all x8, starting transfers between devices: 34.6 us -> 51.6 us  [exchange(): return lax.all_to_all(blocks, axes, 0, 0, tiled=True)]
    ppermute x0 -> x3, starting transfers between devices: none -> 5.81 us  [to_channels_aside(): block = lax.ppermute(block, 'dp', route)]
    ppermute x26, waiting for transfers between devices: 48.9 us -> 54.6 us  [swap_columns(): return lax.ppermute(block, 'pipe', route)]
    ppermute x26, starting transfers between devices: 50.8 us -> 45.7 us  [swap_columns(): return lax.ppermute(block, 'pipe', route)]
    select_n x4 -> x3, other arithmetic: 3.58 us -> 6.85 us  [choose(): return lax.select_n(which, *blocks)]
  transfers between devices with their start and end apart: 43 -> 47, of which waited for: 23 -> 18; matrix products, arithmetic and copies ran while one was open for 18% -> 22% of each run, Pallas kernels for 0% -> 0%
where the time goes in v3:
time: 322 us; the launch traced here: 320 us
  waiting for transfers between devices  132 us (41%)
  starting transfers between devices  110 us (34%)
  other arithmetic  37.1 us (12%)
  local copies, waits for them, and re-layouts  23.8 us (7%)
  matrix products  15.7 us (5%)
    ppermute x26, waiting for transfers between devices, swap_columns(): return lax.ppermute(block, 'pipe', route)  54.6 us
    all_to_all x8, starting transfers between devices, exchange(): return lax.all_to_all(blocks, axes, 0, 0, tiled=True)  51.6 us
    ppermute x26, starting transfers between devices, swap_columns(): return lax.ppermute(block, 'pipe', route)  45.7 us
    ppermute x3, waiting for transfers between devices, all_ranks_aside(): got.append(lax.ppermute(block, 'dp', route))  42.6 us
    ppermute x3, waiting for transfers between devices, to_channels_aside(): block = lax.ppermute(block, 'dp', route)  19.2 us
    dot_general x8, matrix products, dot32(): lax.dot_general(left, right, (dims, ((), ())), preferred_element_type=jnp...  15.4 us
    all_to_all x8, waiting for transfers between devices, exchange(): return lax.all_to_all(blocks, axes, 0, 0, tiled=True)  15.2 us
    select_n x3, other arithmetic, choose(): return lax.select_n(which, *blocks)  6.85 us
  transfers between devices with their start and end apart: 47, of which 18 were waited for; matrix products, arithmetic and copies ran while one was open for 22% of the time, Pallas kernels for 0%

profile of v3, /device:TPU:0, one launch (start us, length us, event | category | flops | bytes accessed | tf_op | source)
XLA Modules:
  0.0 319.9 jit_solution(11780133593184434975)
XLA Ops:
  1.4 3.2 fusion.1
  13.2 6.3 %all-to-all-start = ((bf16[4,64,416]{2,1,0:T(8,128)(2,1)}), bf16[4,64,416]{2,1,0:T(8,128)(2,1)S(1)}, u32[]{:S(2)}, u32[]{:S(2)}) async-start(bf16[4,64,416]{2,1,0:T(8,128)(2,1)} %bitcast.190), calls=%async_computation | async-start | bytes 524288 | tf_op jit(solution)/shard_map/all_to_all | solution.py:47
  22.1 6.3 %all-to-all-done = bf16[4,64,416]{2,1,0:T(8,128)(2,1)S(1)} async-done(((bf16[4,64,416]{2,1,0:T(8,128)(2,1)}), bf16[4,64,416]{2,1,0:T(8,128)(2,1)S(1)}, u32[]{:S(2)}, u32[]{:S(2)}) %all-to-all-start) | async-done | bytes 213024 | tf_op jit(solution)/shard_map/all_to_all | solution.py:47
  28.4 3.0 collective-permute-start.18
  34.2 13.9 %collective-permute-done.10 = bf16[208,896]{1,0:T(8,128)(2,1)S(1)} collective-permute-done((bf16[208,896]{1,0:T(8,128)(2,1)}, bf16[208,896]{1,0:T(8,128)(2,1)S(1)}, u32[]{:S(2)}, u32[]{:S(2)}) %collective-permute-start.10) | collective-permute-done | bytes 372768 | tf_op jit(solution)/shard_map/ppermute | solution.py:72
  50.0 7.6 %collective-permute-done.12 = bf16[208,896]{1,0:T(8,128)(2,1)S(1)} collective-permute-done((bf16[208,896]{1,0:T(8,128)(2,1)}, bf16[208,896]{1,0:T(8,128)(2,1)S(1)}, u32[]{:S(2)}, u32[]{:S(2)}) %collective-permute-start.12) | collective-permute-done | bytes 372768 | tf_op jit(solution)/shard_map/ppermute | solution.py:72
  57.6 3.2 convolution_convert_fusion.2
  60.8 3.5 %all-to-all-start.1 = ((bf16[4,128,896]{2,1,0:T(8,128)(2,1)}), bf16[4,128,896]{2,1,0:T(8,128)(2,1)S(1)}, u32[]{:S(2)}, u32[]{:S(2)}) async-start(bf16[4,128,896]{2,1,0:T(8,128)(2,1)} %bitcast.217), calls=%async_computation.1 | async-start | bytes 1835008 | tf_op jit(solution)/shard_map/all_to_all | solution.py:47
  73.1 12.9 %collective-permute-done = bf16[64,512]{1,0:T(8,128)(2,1)S(1)} collective-permute-done((bf16[64,512]{1,0:T(8,128)(2,1)}, bf16[64,512]{1,0:T(8,128)(2,1)S(1)}, u32[]{:S(2)}, u32[]{:S(2)}) %collective-permute-start) | collective-permute-done | bytes 65568 | tf_op jit(solution)/shard_map/ppermute | solution.py:151
  86.0 6.3 %collective-permute-done.1 = bf16[64,512]{1,0:T(8,128)(2,1)S(1)} collective-permute-done((bf16[64,512]{1,0:T(8,128)(2,1)}, bf16[64,512]{1,0:T(8,128)(2,1)S(1)}, u32[]{:S(2)}, u32[]{:S(2)}) %collective-permute-start.1) | collective-permute-done | bytes 65568 | tf_op jit(solution)/shard_map/ppermute | solution.py:151
  96.2 4.9 %collective-permute-start.3 = (bf16[4,64,512]{2,1,0:T(8,128)(2,1)}, bf16[4,64,512]{2,1,0:T(8,128)(2,1)}, u32[]{:S(2)}, u32[]{:S(2)}) collective-permute-start(bf16[4,64,512]{2,1,0:T(8,128)(2,1)} %pad_maximum_fusion.8), channel_id=1, source_target_pairs={{0,8},{16,24},{1,9},{17,25},{2,10},{18,26},{3,11},{19,27},{4,12},{... | collective-permute-start | bytes 786440 | tf_op jit(solution)/shard_map/ppermute | solution.py:72
  107.3 2.7 fusion.57
  112.2 4.2 %all-to-all-start.2 = ((bf16[4,128,896]{2,1,0:T(8,128)(2,1)}), bf16[4,128,896]{2,1,0:T(8,128)(2,1)}, u32[]{:S(2)}, u32[]{:S(2)}) async-start(bf16[4,128,896]{2,1,0:T(8,128)(2,1)} %broadcast_in_dim.105), calls=%async_computation.2 | async-start | bytes 1835008 | tf_op jit(solution)/shard_map/all_to_all | solution.py:47
  123.6 9.3 %collective-permute-done.20 = bf16[416,896]{1,0:T(8,128)(2,1)} collective-permute-done((bf16[416,896]{1,0:T(8,128)(2,1)S(1)}, bf16[416,896]{1,0:T(8,128)(2,1)}, u32[]{:S(2)}, u32[]{:S(2)}) %collective-permute-start.20) | collective-permute-done | bytes 745504 | tf_op jit(solution)/shard_map/ppermute | solution.py:72
  132.9 5.7 %all-to-all-done.2 = bf16[4,128,896]{2,1,0:T(8,128)(2,1)} async-done(((bf16[4,128,896]{2,1,0:T(8,128)(2,1)}), bf16[4,128,896]{2,1,0:T(8,128)(2,1)}, u32[]{:S(2)}, u32[]{:S(2)}) %all-to-all-start.2) | async-done | bytes 917536 | tf_op jit(solution)/shard_map/all_to_all | solution.py:47
  138.6 2.6 fusion.100
  142.0 3.1 all-to-all-start.3
  153.3 3.5 %collective-permute-done.22 = bf16[256,416]{0,1:T(8,128)(2,1)S(1)} collective-permute-done((bf16[256,416]{0,1:T(8,128)(2,1)S(1)}, bf16[256,416]{0,1:T(8,128)(2,1)S(1)}, u32[]{:S(2)}, u32[]{:S(2)}) %collective-permute-start.22) | collective-permute-done | bytes 213024 | tf_op jit(solution)/shard_map/ppermute | solution.py:72
  156.8 5.3 %collective-permute-done.23 = bf16[256,416]{0,1:T(8,128)(2,1)S(1)} collective-permute-done((bf16[256,416]{0,1:T(8,128)(2,1)S(1)}, bf16[256,416]{0,1:T(8,128)(2,1)S(1)}, u32[]{:S(2)}, u32[]{:S(2)}) %collective-permute-start.23) | collective-permute-done | bytes 213024 | tf_op jit(solution)/shard_map/ppermute | solution.py:72
  162.7 3.3 %select_select_fusion = (bf16[416,896]{1,0:T(8,128)(2,1)}, bf16[416,896]{1,0:T(8,128)(2,1)S(1)}) fusion(bf16[416,896]{1,0:T(8,128)(2,1)} %collective-permute-done.19, bf16[416,896]{1,0:T(8,128)(2,1)} %collective-permute-done.20, bf16[416,896]{1,0:T(8,128)(2,1)} %collective-permute-done.18, pred[]{:T(512)S(6)} %select_n.835, pred[]{:T(512)S(6)} %select_n.770, ...), kind=kLoop, calls=%fused_computation.53 | loop fusion | flops 3354624 | bytes 4474506 | tf_op jit(solution)/shard_map/select_n | solution.py:76
  167.9 4.4 %all-to-all-start.4 = ((bf16[4,128,896]{2,1,0:T(8,128)(2,1)}), bf16[4,128,896]{2,1,0:T(8,128)(2,1)S(1)}, u32[]{:S(2)}, u32[]{:S(2)}) async-start(bf16[4,128,896]{2,1,0:T(8,128)(2,1)} %bitcast.218), calls=%async_computation.4 | async-start | bytes 1835008 | tf_op jit(solution)/shard_map/all_to_all | solution.py:47
  183.6 19.1 %collective-permute-done.26 = bf16[128,1792]{1,0:T(8,128)(2,1)} collective-permute-done((bf16[128,1792]{1,0:T(8,128)(2,1)}, bf16[128,1792]{1,0:T(8,128)(2,1)}, u32[]{:S(2)}, u32[]{:S(2)}) %collective-permute-start.26) | collective-permute-done | bytes 458784 | tf_op jit(solution)/shard_map/ppermute | solution.py:188
  202.7 23.5 %collective-permute-done.27 = bf16[128,1792]{1,0:T(8,128)(2,1)} collective-permute-done((bf16[128,1792]{1,0:T(8,128)(2,1)}, bf16[128,1792]{1,0:T(8,128)(2,1)}, u32[]{:S(2)}, u32[]{:S(2)}) %collective-permute-start.27) | collective-permute-done | bytes 458784 | tf_op jit(solution)/shard_map/ppermute | solution.py:188
  226.2 2.8 pad_maximum_fusion
  230.3 11.7 %all-to-all-start.5 = ((bf16[4,128,896]{2,1,0:T(8,128)(2,1)}), bf16[4,128,896]{2,1,0:T(8,128)(2,1)}, u32[]{:S(2)}, u32[]{:S(2)}) async-start(bf16[4,128,896]{2,1,0:T(8,128)(2,1)} %broadcast_in_dim.109), calls=%async_computation.5 | async-start | bytes 1835008 | tf_op jit(solution)/shard_map/all_to_all | solution.py:47
  252.8 4.1 %collective-permute-start.30 = (bf16[416,896]{1,0:T(8,128)(2,1)}, bf16[416,896]{1,0:T(8,128)(2,1)}, u32[]{:S(2)}, u32[]{:S(2)}) collective-permute-start(bf16[416,896]{1,0:T(8,128)(2,1)} %get-tuple-element.13), channel_id=1, source_target_pairs={{0,8},{16,24},{24,16},{1,9},{17,25},{25,17},{2,10},{18,26},{26,18}... | collective-permute-start | bytes 2236424 | tf_op jit(solution)/shard_map/ppermute | solution.py:72
  256.9 2.7 collective-permute-start.32
  259.6 2.8 collective-permute-start.36
  272.8 9.2 %all-to-all-start.6 = ((bf16[16,16,624]{2,1,0:T(8,128)(2,1)}), bf16[16,16,624]{2,1,0:T(8,128)(2,1)S(1)}, u32[]{:S(2)}, u32[]{:S(2)}) async-start(bf16[16,16,624]{2,1,0:T(8,128)(2,1)} %pad_maximum_fusion.7), calls=%async_computation.6 | async-start | bytes 655360 | tf_op jit(solution)/shard_map/all_to_all | solution.py:47
  287.6 9.1 %collective-permute-done.29 = bf16[416,896]{1,0:T(8,128)(2,1)} collective-permute-done((bf16[416,896]{1,0:T(8,128)(2,1)S(1)}, bf16[416,896]{1,0:T(8,128)(2,1)}, u32[]{:S(2)}, u32[]{:S(2)}) %collective-permute-start.29) | collective-permute-done | bytes 745504 | tf_op jit(solution)/shard_map/ppermute | solution.py:72
  302.3 9.2 %all-to-all-start.7 = ((bf16[4,16,1664]{2,1,0:T(8,128)(2,1)}), bf16[4,16,1664]{2,1,0:T(8,128)(2,1)S(1)}, u32[]{:S(2)}, u32[]{:S(2)}) async-start(bf16[4,16,1664]{2,1,0:T(8,128)(2,1)} %pad_maximum_fusion.9), calls=%async_computation.7 | async-start | bytes 425984 | tf_op jit(solution)/shard_map/all_to_all | solution.py:47
  311.6 3.8 %collective-permute-done.31 = bf16[416,896]{1,0:T(8,128)(2,1)S(1)} collective-permute-done((bf16[416,896]{1,0:T(8,128)(2,1)S(1)}, bf16[416,896]{1,0:T(8,128)(2,1)S(1)}, u32[]{:S(2)}, u32[]{:S(2)}) %collective-permute-start.31) | collective-permute-done | bytes 745504 | tf_op jit(solution)/shard_map/ppermute | solution.py:72
  (234 shorter events, 105.3 us)
Async XLA Ops:
  5.5 22.9 %collective-permute-start.9 = (bf16[208,896]{1,0:T(8,128)(2,1)}, bf16[208,896]{1,0:T(8,128)(2,1)}, u32[]{:S(2)}, u32[]{:S(2)}) collective-permute-start(bf16[208,896]{1,0:T(8,128)(2,1)} %get-tuple-element.25), channel_id=1, source_target_pairs={{24,16},{25,17},{26,18},{27,19},{28,20},{29,21},{30,22},{31,23}} | collective-permute-start | bytes 1118216 | tf_op jit(solution)/shard_map/ppermute | solution.py:72
  7.1 24.4 %collective-permute-start.11 = (bf16[208,896]{1,0:T(8,128)(2,1)}, bf16[208,896]{1,0:T(8,128)(2,1)}, u32[]{:S(2)}, u32[]{:S(2)}) collective-permute-start(bf16[208,896]{1,0:T(8,128)(2,1)} %get-tuple-element.26), channel_id=1, source_target_pairs={{24,8},{25,9},{26,10},{27,11},{28,12},{29,13},{30,14},{31,15}} | collective-permute-start | bytes 1118216 | tf_op jit(solution)/shard_map/ppermute | solution.py:72
  8.5 49.1 %collective-permute-start.13 = (bf16[416,896]{1,0:T(8,128)(2,1)}, bf16[416,896]{1,0:T(8,128)(2,1)}, u32[]{:S(2)}, u32[]{:S(2)}) collective-permute-start(bf16[416,896]{1,0:T(8,128)(2,1)} %get-tuple-element.9), channel_id=1, source_target_pairs={{24,8},{25,9},{26,10},{27,11},{28,12},{29,13},{30,14},{31,15}} | collective-permute-start | bytes 2236424 | tf_op jit(solution)/shard_map/ppermute | solution.py:72
  10.0 47.6 %collective-permute-start.14 = (bf16[416,896]{1,0:T(8,128)(2,1)}, bf16[416,896]{1,0:T(8,128)(2,1)}, u32[]{:S(2)}, u32[]{:S(2)}) collective-permute-start(bf16[416,896]{1,0:T(8,128)(2,1)} %get-tuple-element.8), channel_id=1, source_target_pairs={{24,16},{25,17},{26,18},{27,19},{28,20},{29,21},{30,22},{31,23}} | collective-permute-start | bytes 2236424 | tf_op jit(solution)/shard_map/ppermute | solution.py:72
  13.2 15.3 %all-to-all-start = ((bf16[4,64,416]{2,1,0:T(8,128)(2,1)}), bf16[4,64,416]{2,1,0:T(8,128)(2,1)S(1)}, u32[]{:S(2)}, u32[]{:S(2)}) async-start(bf16[4,64,416]{2,1,0:T(8,128)(2,1)} %bitcast.190), calls=%async_computation | async-start | bytes 524288 | tf_op jit(solution)/shard_map/all_to_all | solution.py:47
  28.4 95.1 %collective-permute-start.18 = (bf16[416,896]{1,0:T(8,128)(2,1)}, bf16[416,896]{1,0:T(8,128)(2,1)}, u32[]{:S(2)}, u32[]{:S(2)}) collective-permute-start(bf16[416,896]{1,0:T(8,128)(2,1)} %get-tuple-element.8), channel_id=1, source_target_pairs={{0,8},{8,0},{16,24},{1,9},{9,1},{17,25},{2,10},{10,2},{18,26},{3,1... | collective-permute-start | bytes 2236424 | tf_op jit(solution)/shard_map/ppermute | solution.py:72
  31.5 16.6 %collective-permute-start.10 = (bf16[208,896]{1,0:T(8,128)(2,1)}, bf16[208,896]{1,0:T(8,128)(2,1)S(1)}, u32[]{:S(2)}, u32[]{:S(2)}) collective-permute-start(bf16[208,896]{1,0:T(8,128)(2,1)} %collective-permute-done.9), channel_id=1, source_target_pairs={{16,0},{17,1},{18,2},{19,3},{20,4},{21,5},{22,6},{23,7}} | collective-permute-start | bytes 1118216 | tf_op jit(solution)/shard_map/ppermute | solution.py:72
  32.8 24.8 %collective-permute-start.12 = (bf16[208,896]{1,0:T(8,128)(2,1)}, bf16[208,896]{1,0:T(8,128)(2,1)S(1)}, u32[]{:S(2)}, u32[]{:S(2)}) collective-permute-start(bf16[208,896]{1,0:T(8,128)(2,1)} %collective-permute-done.11), channel_id=1, source_target_pairs={{8,0},{9,1},{10,2},{11,3},{12,4},{13,5},{14,6},{15,7}} | collective-permute-start | bytes 1118216 | tf_op jit(solution)/shard_map/ppermute | solution.py:72
  48.1 75.4 %collective-permute-start.19 = (bf16[416,896]{1,0:T(8,128)(2,1)}, bf16[416,896]{1,0:T(8,128)(2,1)}, u32[]{:S(2)}, u32[]{:S(2)}) collective-permute-start(bf16[416,896]{1,0:T(8,128)(2,1)} %get-tuple-element.9), channel_id=1, source_target_pairs={{0,16},{8,24},{16,0},{1,17},{9,25},{17,1},{2,18},{10,26},{18,2},{3... | collective-permute-start | bytes 2236424 | tf_op jit(solution)/shard_map/ppermute | solution.py:72
  60.8 49.2 %all-to-all-start.1 = ((bf16[4,128,896]{2,1,0:T(8,128)(2,1)}), bf16[4,128,896]{2,1,0:T(8,128)(2,1)S(1)}, u32[]{:S(2)}, u32[]{:S(2)}) async-start(bf16[4,128,896]{2,1,0:T(8,128)(2,1)} %bitcast.217), calls=%async_computation.1 | async-start | bytes 1835008 | tf_op jit(solution)/shard_map/all_to_all | solution.py:47
  66.0 20.0 %collective-permute-start = (bf16[64,512]{1,0:T(8,128)(2,1)}, bf16[64,512]{1,0:T(8,128)(2,1)S(1)}, u32[]{:S(2)}, u32[]{:S(2)}) collective-permute-start(bf16[64,512]{1,0:T(8,128)(2,1)} %get-tuple-element.64), channel_id=1, source_target_pairs={{0,2},{2,4},{4,6},{6,0},{1,3},{3,5},{5,7},{7,1},{8,10},{10,12},{12... | collective-permute-start | bytes 196616 | tf_op jit(solution)/shard_map/ppermute | solution.py:151
  68.0 24.3 %collective-permute-start.1 = (bf16[64,512]{1,0:T(8,128)(2,1)}, bf16[64,512]{1,0:T(8,128)(2,1)S(1)}, u32[]{:S(2)}, u32[]{:S(2)}) collective-permute-start(bf16[64,512]{1,0:T(8,128)(2,1)} %get-tuple-element.65), channel_id=1, source_target_pairs={{0,4},{2,6},{4,0},{6,2},{1,5},{3,7},{5,1},{7,3},{8,12},{10,14},{12... | collective-permute-start | bytes 196616 | tf_op jit(solution)/shard_map/ppermute | solution.py:151
  70.3 21.9 %collective-permute-start.2 = (bf16[64,512]{1,0:T(8,128)(2,1)}, bf16[64,512]{1,0:T(8,128)(2,1)S(1)}, u32[]{:S(2)}, u32[]{:S(2)}) collective-permute-start(bf16[64,512]{1,0:T(8,128)(2,1)} %get-tuple-element.66), channel_id=1, source_target_pairs={{0,6},{2,0},{4,2},{6,4},{1,7},{3,1},{5,3},{7,5},{8,14},{10,8},{12,... | collective-permute-start | bytes 196616 | tf_op jit(solution)/shard_map/ppermute | solution.py:151
  96.2 20.3 %collective-permute-start.3 = (bf16[4,64,512]{2,1,0:T(8,128)(2,1)}, bf16[4,64,512]{2,1,0:T(8,128)(2,1)}, u32[]{:S(2)}, u32[]{:S(2)}) collective-permute-start(bf16[4,64,512]{2,1,0:T(8,128)(2,1)} %pad_maximum_fusion.8), channel_id=1, source_target_pairs={{0,8},{16,24},{1,9},{17,25},{2,10},{18,26},{3,11},{19,27},{4,12},{... | collective-permute-start | bytes 786440 | tf_op jit(solution)/shard_map/ppermute | solution.py:72
  103.1 15.6 %collective-permute-start.4 = (bf16[4,64,512]{2,1,0:T(8,128)(2,1)}, bf16[4,64,512]{2,1,0:T(8,128)(2,1)}, u32[]{:S(2)}, u32[]{:S(2)}) collective-permute-start(bf16[4,64,512]{2,1,0:T(8,128)(2,1)} %pad_maximum_fusion.8), channel_id=1, source_target_pairs={{0,16},{16,0},{1,17},{17,1},{2,18},{18,2},{3,19},{19,3},{4,20},{20... | collective-permute-start | bytes 786440 | tf_op jit(solution)/shard_map/ppermute | solution.py:72
  112.2 26.4 %all-to-all-start.2 = ((bf16[4,128,896]{2,1,0:T(8,128)(2,1)}), bf16[4,128,896]{2,1,0:T(8,128)(2,1)}, u32[]{:S(2)}, u32[]{:S(2)}) async-start(bf16[4,128,896]{2,1,0:T(8,128)(2,1)} %broadcast_in_dim.105), calls=%async_computation.2 | async-start | bytes 1835008 | tf_op jit(solution)/shard_map/all_to_all | solution.py:47
  116.5 16.4 %collective-permute-start.20 = (bf16[416,896]{1,0:T(8,128)(2,1)S(1)}, bf16[416,896]{1,0:T(8,128)(2,1)}, u32[]{:S(2)}, u32[]{:S(2)}) collective-permute-start(bf16[416,896]{1,0:T(8,128)(2,1)S(1)} %get-tuple-element.10), channel_id=1, source_target_pairs={{0,24},{8,16},{16,8},{1,25},{9,17},{17,9},{2,26},{10,18},{18,10},{... | collective-permute-start | bytes 2236424 | tf_op jit(solution)/shard_map/ppermute | solution.py:72
  120.6 61.4 %collective-permute-start.6 = (bf16[4,64,512]{2,1,0:T(8,128)(2,1)}, bf16[4,64,512]{2,1,0:T(8,128)(2,1)}, u32[]{:S(2)}, u32[]{:S(2)}) collective-permute-start(bf16[4,64,512]{2,1,0:T(8,128)(2,1)} %get-tuple-element.18), channel_id=1, source_target_pairs={{0,1},{1,0},{2,3},{3,2},{4,5},{5,4},{6,7},{7,6},{8,9},{9,8},{10,11... | collective-permute-start | bytes 786440 | tf_op jit(solution)/shard_map/ppermute | solution.py:51
  167.9 61.1 %all-to-all-start.4 = ((bf16[4,128,896]{2,1,0:T(8,128)(2,1)}), bf16[4,128,896]{2,1,0:T(8,128)(2,1)S(1)}, u32[]{:S(2)}, u32[]{:S(2)}) async-start(bf16[4,128,896]{2,1,0:T(8,128)(2,1)} %bitcast.218), calls=%async_computation.4 | async-start | bytes 1835008 | tf_op jit(solution)/shard_map/all_to_all | solution.py:47
  173.1 29.6 %collective-permute-start.26 = (bf16[128,1792]{1,0:T(8,128)(2,1)}, bf16[128,1792]{1,0:T(8,128)(2,1)}, u32[]{:S(2)}, u32[]{:S(2)}) collective-permute-start(bf16[128,1792]{1,0:T(8,128)(2,1)} %pad_maximum_fusion.4), channel_id=1, source_target_pairs={{0,2},{2,4},{4,6},{6,0},{1,3},{3,5},{5,7},{7,1},{8,10},{10,12},{12... | collective-permute-start | bytes 1376264 | tf_op jit(solution)/shard_map/ppermute | solution.py:188
  175.1 51.1 %collective-permute-start.27 = (bf16[128,1792]{1,0:T(8,128)(2,1)}, bf16[128,1792]{1,0:T(8,128)(2,1)}, u32[]{:S(2)}, u32[]{:S(2)}) collective-permute-start(bf16[128,1792]{1,0:T(8,128)(2,1)} %pad_maximum_fusion.4), channel_id=1, source_target_pairs={{0,4},{2,6},{4,0},{6,2},{1,5},{3,7},{5,1},{7,3},{8,12},{10,14},{12... | collective-permute-start | bytes 1376264 | tf_op jit(solution)/shard_map/ppermute | solution.py:188
  177.5 48.7 %collective-permute-start.28 = (bf16[128,1792]{1,0:T(8,128)(2,1)}, bf16[128,1792]{1,0:T(8,128)(2,1)}, u32[]{:S(2)}, u32[]{:S(2)}) collective-permute-start(bf16[128,1792]{1,0:T(8,128)(2,1)} %pad_maximum_fusion.4), channel_id=1, source_target_pairs={{0,6},{2,0},{4,2},{6,4},{1,7},{3,1},{5,3},{7,5},{8,14},{10,8},{12,... | collective-permute-start | bytes 1376264 | tf_op jit(solution)/shard_map/ppermute | solution.py:188
  230.3 34.0 %all-to-all-start.5 = ((bf16[4,128,896]{2,1,0:T(8,128)(2,1)}), bf16[4,128,896]{2,1,0:T(8,128)(2,1)}, u32[]{:S(2)}, u32[]{:S(2)}) async-start(bf16[4,128,896]{2,1,0:T(8,128)(2,1)} %broadcast_in_dim.109), calls=%async_computation.5 | async-start | bytes 1835008 | tf_op jit(solution)/shard_map/all_to_all | solution.py:47
  252.8 32.2 %collective-permute-start.30 = (bf16[416,896]{1,0:T(8,128)(2,1)}, bf16[416,896]{1,0:T(8,128)(2,1)}, u32[]{:S(2)}, u32[]{:S(2)}) collective-permute-start(bf16[416,896]{1,0:T(8,128)(2,1)} %get-tuple-element.13), channel_id=1, source_target_pairs={{0,8},{16,24},{24,16},{1,9},{17,25},{25,17},{2,10},{18,26},{26,18}... | collective-permute-start | bytes 2236424 | tf_op jit(solution)/shard_map/ppermute | solution.py:72
  256.9 54.7 %collective-permute-start.32 = (bf16[416,896]{1,0:T(8,128)(2,1)}, bf16[416,896]{1,0:T(8,128)(2,1)}, u32[]{:S(2)}, u32[]{:S(2)}) collective-permute-start(bf16[416,896]{1,0:T(8,128)(2,1)} %get-tuple-element.12), channel_id=1, source_target_pairs={{0,16},{8,24},{24,8},{1,17},{9,25},{25,9},{2,18},{10,26},{26,10},{... | collective-permute-start | bytes 2236424 | tf_op jit(solution)/shard_map/ppermute | solution.py:72
  259.6 57.2 %collective-permute-start.36 = (bf16[416,896]{1,0:T(8,128)(2,1)}, bf16[416,896]{1,0:T(8,128)(2,1)}, u32[]{:S(2)}, u32[]{:S(2)}) collective-permute-start(bf16[416,896]{1,0:T(8,128)(2,1)} %get-tuple-element.11), channel_id=1, source_target_pairs={{0,24},{8,16},{16,8},{1,25},{9,17},{17,9},{2,26},{10,18},{18,10},{... | collective-permute-start | bytes 2236424 | tf_op jit(solution)/shard_map/ppermute | solution.py:72
  268.2 28.5 %collective-permute-start.29 = (bf16[416,896]{1,0:T(8,128)(2,1)S(1)}, bf16[416,896]{1,0:T(8,128)(2,1)}, u32[]{:S(2)}, u32[]{:S(2)}) collective-permute-start(bf16[416,896]{1,0:T(8,128)(2,1)S(1)} %convolution_convert_fusion.6), channel_id=1, source_target_pairs={{8,0},{9,1},{10,2},{11,3},{12,4},{13,5},{14,6},{15,7}} | collective-permute-start | bytes 2236424 | tf_op jit(solution)/shard_map/ppermute | solution.py:72
  270.4 15.9 %collective-permute-start.34 = (bf16[208,896]{1,0:T(8,128)(2,1)}, bf16[208,896]{1,0:T(8,128)(2,1)}, u32[]{:S(2)}, u32[]{:S(2)}) collective-permute-start(bf16[208,896]{1,0:T(8,128)(2,1)} %get-tuple-element.24), channel_id=1, source_target_pairs={{24,8},{25,9},{26,10},{27,11},{28,12},{29,13},{30,14},{31,15}} | collective-permute-start | bytes 1118216 | tf_op jit(solution)/shard_map/ppermute | solution.py:72
  272.8 27.4 %all-to-all-start.6 = ((bf16[16,16,624]{2,1,0:T(8,128)(2,1)}), bf16[16,16,624]{2,1,0:T(8,128)(2,1)S(1)}, u32[]{:S(2)}, u32[]{:S(2)}) async-start(bf16[16,16,624]{2,1,0:T(8,128)(2,1)} %pad_maximum_fusion.7), calls=%async_computation.6 | async-start | bytes 655360 | tf_op jit(solution)/shard_map/all_to_all | solution.py:47
  285.0 30.3 %collective-permute-start.31 = (bf16[416,896]{1,0:T(8,128)(2,1)S(1)}, bf16[416,896]{1,0:T(8,128)(2,1)S(1)}, u32[]{:S(2)}, u32[]{:S(2)}) collective-permute-start(bf16[416,896]{1,0:T(8,128)(2,1)S(1)} %convolution_convert_fusion.6), channel_id=1, source_target_pairs={{16,0},{17,1},{18,2},{19,3},{20,4},{21,5},{22,6},{23,7}} | collective-permute-start | bytes 2236424 | tf_op jit(solution)/shard_map/ppermute | solution.py:72
  286.3 30.5 %collective-permute-start.33 = (bf16[208,896]{1,0:T(8,128)(2,1)}, bf16[208,896]{1,0:T(8,128)(2,1)S(1)}, u32[]{:S(2)}, u32[]{:S(2)}) collective-permute-start(bf16[208,896]{1,0:T(8,128)(2,1)} %get-tuple-element.23), channel_id=1, source_target_pairs={{24,0},{25,1},{26,2},{27,3},{28,4},{29,5},{30,6},{31,7}} | collective-permute-start | bytes 1118216 | tf_op jit(solution)/shard_map/ppermute | solution.py:72
  296.7 20.1 %collective-permute-start.35 = (bf16[208,896]{1,0:T(8,128)(2,1)}, bf16[208,896]{1,0:T(8,128)(2,1)}, u32[]{:S(2)}, u32[]{:S(2)}) collective-permute-start(bf16[208,896]{1,0:T(8,128)(2,1)} %collective-permute-done.34), channel_id=1, source_target_pairs={{8,0},{9,1},{10,2},{11,3},{12,4},{13,5},{14,6},{15,7}} | collective-permute-start | bytes 1118216 | tf_op jit(solution)/shard_map/ppermute | solution.py:72
  (37 other events, 346.6 us)
